TPU v7x, 32 devices: a whole 2x2x4 slice. The times are simulated.
32 devices in a mesh: col: 8 (over z, x), row: 4 (over y, core).
Axes of the slice: x: 2, y: 2, z: 4, core: 2. Of those that a mesh axis runs over, the one named last changes fastest.
Arguments:
- weight: float32 [8192, 16384], P('row', 'col'), may hold values from -6 to 6
- momentum: float32 [8192, 16384], P('row', 'col'), may hold values from -6 to 6
- gradient: bfloat16 [8192, 16384], P('row', 'col'), may hold values from -6 to 6
- right_factor: float32 [16384, 256], P('col'), may hold values from -6 to 6
Outputs:
- new_weight: float32 [8192, 16384], P('row', 'col')
- new_momentum: float32 [8192, 16384], P('row', 'col')
- new_factor: float32 [16384, 256], P('col')
All inputs are finite; a program needn't handle non-finite values.
Results may differ from a plain program's by a relative error of at most 0.0003.
Values sent between devices are 32-bit elements; how exact they have to be, the bound alone decides.
No kernel may reach another device: no remote copies, remote signals or barrier semaphores. Data moves between devices by JAX's collectives and lax.ppermute only.
A program may use at most 128 MiB of HBM per device.

v0:
```python
import jax
import jax.numpy as jnp
from jax import lax
from jax.sharding import PartitionSpec as P

D_IN = 16384


def contract(first, second, first_dim, second_dim):
    return lax.dot_general(
        first,
        second,
        (((first_dim,), (second_dim,)), ((), ())),
        precision=lax.Precision.HIGHEST,
        preferred_element_type=jnp.float32,
    )


def orthonormal(left_raw, gram_matrix):
    lower = jnp.linalg.cholesky(gram_matrix)
    return lax.linalg.triangular_solve(
        lower, left_raw, left_side=False, lower=True, transpose_a=True
    )


def on_device(weight, momentum, gradient, right_factor):
    combined = momentum + gradient.astype(jnp.float32)
    partial_value = contract(combined, right_factor, 1, 0)
    left_raw = lax.psum(partial_value, "col")
    gram_matrix = lax.psum(contract(left_raw, left_raw, 0, 0), "row")
    left_factor = orthonormal(left_raw, gram_matrix)
    right_raw = lax.psum(contract(combined, left_factor, 0, 0), "row")
    squares = lax.psum(jnp.sum(right_raw * right_raw, axis=0), "col")
    new_factor = right_raw / jnp.sqrt(squares / D_IN + 1e-06)
    new_momentum = combined - 0.05 * contract(left_factor, right_raw, 1, 1)
    new_weight = weight - 0.5 * contract(left_factor, new_factor, 1, 1)
    return (new_weight, new_momentum, new_factor)


def solution(mesh):
    in_specs = (P("row", "col"), P("row", "col"), P("row", "col"), P("col", None))
    out_specs = (P("row", "col"), P("row", "col"), P("col", None))
    return jax.shard_map(
        on_device, mesh=mesh, in_specs=in_specs, out_specs=out_specs, check_vma=False
    )
```

profile of v0, /device:TPU:0, one launch (start us, length us, event | category | flops | bytes accessed | tf_op | source)
XLA Modules:
  0.0 417.5 jit_solution(15536495732991310134)
XLA Ops:
  7.2 1.5 copy-done
  8.8 18.3 %fusion.1 = f32[2048,256]{1,0:T(8,128)} fusion(f32[2048,256]{1,0:T(8,128)S(1)} %copy-done, f32[2048,2048]{1,0:T(8,128)} %param.5, bf16[2048,2048]{1,0:T(8,128)(2,1)} %param.6), kind=kOutput, calls=%fused_computation.6 | convolution fusion | flops 12893290496 | bytes 29360128 | tf_op jit(solution)/shard_map/dot_general | solution.py:10
  27.1 105.1 %all-reduce.5.cloned.1.call-done = f32[2048,256]{1,0:T(8,128)} async-done(((f32[2048,256]{1,0:T(8,128)}), f32[2048,256]{1,0:T(8,128)}) %all-reduce.5.cloned.1.call-update) | async-done | bytes 2097168 | tf_op jit(solution)/shard_map/psum | solution.py:29
  132.2 6.4 %fusion.14 = f32[256,256]{0,1:T(8,128)} fusion(f32[2048,256]{1,0:T(8,128)} %all-reduce.5.cloned.1.call-done), kind=kOutput, calls=%fused_computation.40 | convolution fusion | flops 1610612736 | bytes 2359296 | tf_op jit(solution)/shard_map/dot_general | solution.py:10
  138.6 0.6 all-reduce.9.cloned.1.call-start
  139.2 31.1 %all-reduce.7.cloned.1.call-done = f32[256,256]{0,1:T(8,128)} async-done(((f32[256,256]{0,1:T(8,128)}), f32[256,256]{0,1:T(8,128)}) %all-reduce.7.cloned.1.call-update) | async-done | bytes 262160 | tf_op jit(solution)/shard_map/psum | solution.py:30
  170.3 1.1 copy.8
  171.4 1.0 fusion.4
  172.4 11.7 %cholesky.50 = f32[128,128]{1,0:T(8,128)S(1)} custom-call(f32[128,128]{1,0:T(8,128)S(1)} %cholesky.118), custom_call_target="Cholesky" | custom-call | tf_op jit(solution)/shard_map/jit(cholesky)/cholesky | solution.py:20
  184.2 9.8 %custom-call.14 = f32[1,128,128]{1,2,0:T(8,128)S(1)} custom-call(f32[1,128,128]{2,1,0:T(8,128)S(1)} %get-tuple-element.24), custom_call_target="InvertDiagBlocksLowerTriangular" | custom-call | tf_op jit(solution)/shard_map/jit(cholesky)/cholesky | solution.py:20
  194.0 0.2 constant_dynamic-update-slice_fusion.1
  194.2 0.3 convolution_subtract_fusion.1
  194.5 11.7 %cholesky.105 = f32[128,128]{1,0:T(8,128)S(1)} custom-call(f32[128,128]{1,0:T(8,128)S(1)} %convolution_subtract_fusion.1), custom_call_target="Cholesky" | custom-call | tf_op jit(solution)/shard_map/jit(cholesky)/cholesky | solution.py:20
  206.3 0.6 compare_reduce_fusion
  208.3 4.2 while.1
  208.5 0.6 fusion.25
  209.1 1.4 bitcast_dynamic-update-slice_fusion.2
  210.5 0.6 fusion.25
  211.1 1.4 bitcast_dynamic-update-slice_fusion.2
  212.5 19.7 %custom-call.15 = f32[2,128,128]{1,2,0:T(8,128)S(1)} custom-call(f32[2,128,128]{2,1,0:T(8,128)S(1)} %get-tuple-element.10), custom_call_target="InvertDiagBlocksLowerTriangular" | custom-call | tf_op jit(solution)/shard_map/triangular_solve | solution.py:21
  232.2 1.1 fusion.2
  233.2 1.8 convolution_subtract_fusion
  235.1 1.1 fusion.5
  236.2 32.4 %fusion = f32[2048,256]{1,0:T(8,128)} fusion(f32[2048,2048]{1,0:T(8,128)} %param.5, bf16[2048,2048]{1,0:T(8,128)(2,1)} %param.6, f32[2048,128]{0,1:T(8,128)S(1)} %fusion.5, f32[2048,128]{0,1:T(8,128)S(1)} %fusion.2), kind=kOutput, calls=%fused_computation.5 | convolution fusion | flops 12893814784 | bytes 29360128 | tf_op jit(solution)/shard_map/dot_general | solution.py:10
  268.6 51.5 %all-reduce.9.cloned.1.call-done = f32[2048,256]{1,0:T(8,128)} async-done(((f32[2048,256]{1,0:T(8,128)}), f32[2048,256]{1,0:T(8,128)}) %all-reduce.9.cloned.1.call-update) | async-done | bytes 2097168 | tf_op jit(solution)/shard_map/psum | solution.py:32
  320.2 2.0 multiply_reduce_fusion
  322.2 21.3 %psum.31 = f32[256]{0:T(256)S(1)} all-reduce(f32[256]{0:T(256)S(1)} %multiply_reduce_fusion), channel_id=1, replica_groups=mesh['col'=8,'row'=4] {'col'}, use_global_device_ids=true, to_apply=%region_8.9 | all-reduce | flops 256 | bytes 2048 | tf_op jit(solution)/shard_map/psum | solution.py:33
  343.6 0.1 broadcast_divide_fusion
  343.7 1.3 copy-done.7
  345.1 0.1 copy-done.6
  345.2 31.9 %multiply_subtract_fusion.1 = f32[2048,2048]{1,0:T(8,128)} fusion(f32[2048,2048]{1,0:T(8,128)} %param.4, f32[2048,256]{1,0:T(8,128)S(1)} %broadcast_divide_fusion, f32[2048,128]{0,1:T(8,128)S(1)} %copy-done.6, f32[2048,128]{0,1:T(8,128)S(1)} %fusion.2), kind=kOutput, calls=%fused_computation.3 | convolution fusion | flops 12893814784 | bytes 37748736 | tf_op jit(solution)/shard_map/dot_general | solution.py:10
  377.1 33.4 %multiply_subtract_fusion = f32[2048,2048]{1,0:T(8,128)} fusion(f32[2048,256]{1,0:T(8,128)S(1)} %copy-done.4, f32[2048,2048]{1,0:T(8,128)} %param.5, bf16[2048,2048]{1,0:T(8,128)(2,1)} %param.6, f32[2048,128]{0,1:T(8,128)S(1)} %copy-done.6, f32[2048,128]{0,1:T(8,128)S(1)} %fusion.2), kind=kOutput, calls=%fused_computation.2 | convolution fusion | flops 12902203392 | bytes 46137344 | tf_op jit(solution)/shard_map/dot_general | solution.py:10
  (29 shorter events, 0.4 us)
Async XLA Ops:
  7.2 1.6 copy-start
  7.2 125.0 %all-reduce.5.cloned.1.call-start = ((), (), s32[]{:S(2)}) async-start(), calls=%async_computation | async-start | bytes 4194304 | tf_op jit(solution)/shard_map/psum | solution.py:29
  27.0 143.3 %all-reduce.7.cloned.1.call-start = ((), (), s32[]{:S(2)}) async-start(), calls=%async_computation.1 | async-start | bytes 524288 | tf_op jit(solution)/shard_map/psum | solution.py:30
  138.6 93.5 %copy-start.2 = (f32[2048,256]{1,0:T(8,128)S(1)}, f32[2048,256]{1,0:T(8,128)}, u32[]{:S(2)}) copy-start(f32[2048,256]{1,0:T(8,128)} %all-reduce.5.cloned.1.call-done) | copy-start | bytes 6291460
  138.6 181.5 %all-reduce.9.cloned.1.call-start = ((), (), s32[]{:S(2)}) async-start(), calls=%async_computation.2 | async-start | bytes 4194304 | tf_op jit(solution)/shard_map/psum | solution.py:32
  236.2 32.5 %copy-start.5 = (f32[2048,128]{0,1:T(8,128)}, f32[2048,128]{0,1:T(8,128)S(1)}, u32[]{:S(2)}) copy-start(f32[2048,128]{0,1:T(8,128)S(1)} %fusion.5) | copy-start | bytes 3145732
  320.2 23.4 %copy-start.3 = (f32[2048,256]{1,0:T(8,128)S(1)}, f32[2048,256]{1,0:T(8,128)}, u32[]{:S(2)}) copy-start(f32[2048,256]{1,0:T(8,128)} %all-reduce.9.cloned.1.call-done) | copy-start | bytes 6291460
  343.6 1.6 copy-start.6
  343.7 1.3 copy-start.7
  345.2 31.9 %copy-start.4 = (f32[2048,256]{1,0:T(8,128)S(1)}, f32[2048,256]{1,0:T(8,128)}, u32[]{:S(2)}) copy-start(f32[2048,256]{1,0:T(8,128)} %all-reduce.9.cloned.1.call-done) | copy-start | bytes 6291460
  377.1 33.4 %copy-start.1 = (f32[2048,256]{1,0:T(8,128)S(1)}, f32[2048,256]{1,0:T(8,128)}, u32[]{:S(2)}) copy-start(f32[2048,256]{1,0:T(8,128)} %param.7) | copy-start | bytes 6291460
Sparse Core Ops, SparseCore 0:
  27.2 105.0 all-reduce.4
  138.8 31.5 all-reduce.6
  268.8 51.3 all-reduce.8
where the time goes:
time: 424 us; the launch traced here: 418 us
  waiting for transfers between devices  188 us (44%)
  matrix products  127 us (30%)
  other arithmetic  56.8 us (13%)
  blocking collectives  21.3 us (5%)
  between operations  15.7 us (4%)
  local copies, waits for them, and re-layouts  8.11 us (2%)
    dot_general x5, matrix products, contract(): lax.dot_general(first, second, (((first_dim,), (second_dim,)), ((), ())),...  122 us
    psum x1, waiting for transfers between devices, on_device(): left_raw = lax.psum(partial_value, 'col')  105 us
    psum x1, waiting for transfers between devices, on_device(): right_raw = lax.psum(contract(combined, left_factor, 0, 0), 'row')  51.5 us
    another operation x6, other arithmetic, orthonormal(): lower = jnp.linalg.cholesky(gram_matrix)  34 us
    psum x1, waiting for transfers between devices, on_device(): gram_matrix = lax.psum(contract(left_raw, left_raw, 0, 0), 'row')  31.1 us
    psum x1, blocking collectives, on_device(): squares = lax.psum(jnp.sum(right_raw * right_raw, axis=0), 'col')  21.3 us
    another operation x3, other arithmetic, orthonormal(): lax.linalg.triangular_solve(lower, left_raw, left_side=False, lower=True,...  19.7 us
  transfers between devices with their start and end apart: 3, of which 3 were waited for; matrix products, arithmetic and copies ran while one was open for 0% of the time, Pallas kernels for 0%

commit v1 on v0

v1 whole, which is shorter than its diff:
```python
import functools

import jax
import jax.numpy as jnp
from jax import lax
from jax.experimental import pallas as pl
from jax.experimental.pallas import tpu as pltpu
from jax.sharding import PartitionSpec as P


F32, BF16 = jnp.float32, jnp.bfloat16
HIGHEST = lax.Precision.HIGHEST
NN = (((1,), (0,)), ((), ()))
TN = (((0,), (0,)), ((), ()))
NT = (((1,), (1,)), ((), ()))


def dot(first, second, dims, precision=None):
    return lax.dot_general(first, second, dims, precision=precision, preferred_element_type=F32)


def halves(value):
    high = value.astype(BF16)
    return high, (value - high.astype(F32)).astype(BF16)


def call(kernel, flops, nbytes, limit=16, **kwargs):
    return pl.pallas_call(
        kernel,
        cost_estimate=pl.CostEstimate(flops=flops, bytes_accessed=nbytes, transcendentals=0),
        compiler_params=pltpu.CompilerParams(vmem_limit_bytes=limit << 20),
        **kwargs,
    )


def tile(rows, most=256):
    return min(rows, most)


def fixed(i):
    return (0, 0)


def near_core(value):
    return pltpu.with_memory_space_constraint(value, pltpu.VMEM)


def in_hbm(value):
    return pltpu.with_memory_space_constraint(value, pltpu.HBM)


RESIDENT = pl.BlockSpec(memory_space=pltpu.VMEM)


def along(value, axis):
    high, low = halves(value)
    return jnp.concatenate([high, high, low], axis=axis)


def along_swapped(value, axis):
    high, low = halves(value)
    return jnp.concatenate([high, low, high], axis=axis)


def left_kernel(opening, m_ref, g_ref, r_ref, p_ref, c_ref, *refs):
    i = pl.program_id(0)
    split_ref = refs[0] if opening else r_ref
    if opening:

        @pl.when(i == 0)
        def _():
            split_ref[...] = along_swapped(r_ref[...], 0)

    combined = m_ref[...] + g_ref[...].astype(F32)
    c_ref[...] = combined
    p_ref[...] = dot(along(combined, 1), split_ref[...], NN)


def left_part(momentum, gradient, right, opening, start, rows):
    n = momentum.shape[1]
    rank = right.shape[1]
    bm = tile(rows)
    first = start // bm
    block = pl.BlockSpec((bm, n), lambda i: (i + first, 0))
    here = lambda i: (i, 0)
    out_specs = [pl.BlockSpec((bm, rank), here), pl.BlockSpec((bm, n), here)]
    out_shape = [jax.ShapeDtypeStruct((rows, rank), F32), pltpu.HBM((rows, n), F32)]
    if opening:
        out_specs.append(RESIDENT)
        out_shape.append(pltpu.VMEM((3 * n, rank), BF16))
        right, spec = in_hbm(right), pl.BlockSpec((n, rank), fixed)
    else:
        right, spec = near_core(right), RESIDENT
    return call(
        functools.partial(left_kernel, opening), 6 * rows * n * rank, rows * n * 6,
        grid=(rows // bm,),
        in_specs=[block, block, spec],
        out_specs=tuple(out_specs),
        out_shape=tuple(out_shape),
    )(in_hbm(momentum), in_hbm(gradient), right)


def cross_kernel(l_ref, c_ref, *refs):
    acc = refs[-1]
    n = c_ref.shape[1]
    left = along(l_ref[...].T, 1)
    step = min(n, 512)
    for c in range(0, n, step):
        value = dot(left, along_swapped(c_ref[:, c : c + step], 0), NN)
        acc[:, c : c + step] = value + refs[0][:, c : c + step] if len(refs) > 1 else value


def cross_part(left, combined, before):
    rows, rank = left.shape
    n = combined.shape[1]
    extra = [] if before is None else [before]
    return call(
        cross_kernel, 6 * rows * n * rank, rank * n * 8,
        in_specs=[RESIDENT] * (2 + len(extra)),
        out_specs=RESIDENT,
        out_shape=jax.ShapeDtypeStruct((rank, n), F32),
        input_output_aliases={2: 0} if extra else {},
    )(left, near_core(combined), *extra)


def gram_kernel(*refs):
    left = refs[0][...]
    value = dot(left, left, TN, HIGHEST)
    refs[-1][...] = value + refs[1][...] if len(refs) > 2 else value


def gram_part(left, before):
    rows, rank = left.shape
    extra = [] if before is None else [before]
    return call(
        gram_kernel, 12 * rows * rank * rank, rows * rank * 4,
        out_shape=jax.ShapeDtypeStruct((rank, rank), F32),
    )(left, *extra)


def inverse_kernel(g_ref, x_ref, work):
    rank = g_ref.shape[0]
    b = min(32, rank)
    rows = lax.broadcasted_iota(jnp.int32, (rank, rank), 0)
    cols = lax.broadcasted_iota(jnp.int32, (rank, rank), 1)
    work[:, :rank] = g_ref[...]
    work[:, rank:] = jnp.where(rows == cols, 1.0, 0.0).astype(F32)
    r = lax.broadcasted_iota(jnp.int32, (b, b), 0)
    c = lax.broadcasted_iota(jnp.int32, (b, b), 1)
    for j in range(0, rank, b):
        block = work[j : j + b, j : j + b]
        inv = jnp.where(r == c, 1.0, 0.0).astype(F32)
        aug = jnp.concatenate([block, inv], axis=1)
        sub = lax.broadcasted_iota(jnp.int32, (b, 2 * b), 0)
        pivots = jnp.zeros((b, 1), F32)
        for i in range(b):
            pivot = aug[i : i + 1, i : i + 1]
            row = aug[i : i + 1, :] * (1.0 / pivot)
            col = jnp.where(sub[:, :1] > i, aug[:, i : i + 1], 0.0)
            pivots = jnp.where(sub[:, :1] == i, pivot, pivots)
            aug = aug - col * row
        inv = aug[:, b:] * lax.rsqrt(pivots)
        panel = dot(inv, work[j : j + b, :], NN, HIGHEST)
        work[j : j + b, :] = panel
        if j + b < rank:
            work[j + b :, :] -= dot(panel[:, j + b : rank], panel, TN, HIGHEST)
    x_ref[...] = work[:, rank:]


def inverse_factor(gram):
    rank = gram.shape[0]
    return call(
        inverse_kernel, 12 * rank**3 * 20, rank * rank * 8,
        out_shape=jax.ShapeDtypeStruct((rank, rank), F32),
        scratch_shapes=[pltpu.VMEM((rank, 2 * rank), F32)],
    )(gram)


def basis_kernel(l_ref, x_ref, o_ref):
    o_ref[...] = dot(l_ref[...], x_ref[...], NT, HIGHEST)


def basis(left, inverse):
    rows, rank = left.shape
    return call(
        basis_kernel, 12 * rows * rank * rank, rows * rank * 8,
        out_shape=jax.ShapeDtypeStruct((rows, rank), F32),
    )(left, inverse)


def right_kernel(x_ref, z_ref, o_ref, s_ref):
    value = dot(x_ref[...], z_ref[...], NN, HIGHEST)
    o_ref[...] = value
    s_ref[...] = jnp.broadcast_to(jnp.sum(value * value, axis=1, keepdims=True), s_ref.shape)


def right_side(inverse, cross):
    rank, n = cross.shape
    return call(
        right_kernel, 12 * n * rank * rank, n * rank * 8,
        out_shape=(jax.ShapeDtypeStruct((rank, n), F32), jax.ShapeDtypeStruct((rank, 128), F32)),
    )(inverse, cross)


def momentum_kernel(parts, half_ref, l_ref, r_ref, *refs):
    o_ref, split = refs[-2:]
    i = pl.program_id(0)
    _, width = o_ref.shape

    @pl.when(i == 0)
    def _():
        high, low = halves(r_ref[...])
        split[...] = jnp.concatenate([high, low], axis=0)

    left = l_ref[...].astype(BF16)
    update = dot(jnp.concatenate([left, left], axis=1), split[...], NN)
    columns = pl.ds(pl.multiple_of(half_ref[0] * width, width), width)
    for part in range(parts):

        @pl.when(i == part)
        def _():
            o_ref[...] = refs[part][:, columns] - 0.05 * update


def momentum_half(half, left, right, parts, first, before):
    rows, rank = left.shape
    width = right.shape[1]
    bm = parts[0].shape[0]
    extra = [] if before is None else [before]
    n_in = 3 + len(parts) + len(extra)
    return pl.pallas_call(
        functools.partial(momentum_kernel, len(parts)),
        name="momentum",
        cost_estimate=pl.CostEstimate(flops=4 * bm * len(parts) * width * rank, bytes_accessed=bm * len(parts) * width * 4, transcendentals=0),
        compiler_params=pltpu.CompilerParams(vmem_limit_bytes=16 << 20),
        grid_spec=pltpu.PrefetchScalarGridSpec(
            num_scalar_prefetch=1,
            grid=(len(parts),),
            in_specs=[
                pl.BlockSpec((bm, rank), lambda i, half: (i + first, 0)),
                pl.BlockSpec((rank, width), lambda i, half: (0, 0)),
            ] + [RESIDENT] * len(parts) + [pl.BlockSpec(memory_space=pl.ANY)] * len(extra),
            out_specs=pl.BlockSpec((bm, width), lambda i, half: (i + first, half[0])),
            scratch_shapes=[pltpu.VMEM((2 * rank, width), BF16)],
        ),
        out_shape=jax.ShapeDtypeStruct((rows, 2 * width), F32),
        input_output_aliases={n_in - 1: 0} if extra else {},
    )(half, left, right, *[near_core(part) for part in parts], *extra)


def weight_kernel(count, half_ref, l_ref, a_ref, b_ref, s_ref, w_ref, o_ref, f_ref, split):
    @pl.when(pl.program_id(0) == 0)
    def _():
        scale = jnp.sqrt(s_ref[:, :1] / count + 1e-06)
        width = a_ref.shape[1]
        for side, ref in ((half_ref[0], a_ref), (1 - half_ref[0], b_ref)):
            factor = ref[...] / scale
            start = pl.multiple_of(side * width, width)
            split[:, pl.ds(start, width)] = along_swapped(factor, 0)
            f_ref[pl.ds(start, width), :] = factor.T

    update = dot(along(l_ref[...], 1), split[...], NN)
    o_ref[...] = w_ref[...] - 0.5 * update


def weight_update(half, left, own, other, squares, weight, count):
    rows, n = weight.shape
    rank, width = own.shape
    bm = tile(rows)
    row = lambda i, half: (i, 0)
    still = lambda i, half: (0, 0)
    return pl.pallas_call(
        functools.partial(weight_kernel, float(count)),
        name="weight",
        cost_estimate=pl.CostEstimate(flops=6 * rows * n * rank, bytes_accessed=rows * n * 8, transcendentals=0),
        compiler_params=pltpu.CompilerParams(vmem_limit_bytes=16 << 20),
        grid_spec=pltpu.PrefetchScalarGridSpec(
            num_scalar_prefetch=1,
            grid=(rows // bm,),
            in_specs=[
                pl.BlockSpec((bm, rank), row),
                pl.BlockSpec((rank, width), still),
                pl.BlockSpec((rank, width), still),
                pl.BlockSpec(squares.shape, still),
                pl.BlockSpec((bm, n), row),
            ],
            out_specs=(pl.BlockSpec((bm, n), row), pl.BlockSpec((n, rank), still)),
            scratch_shapes=[pltpu.VMEM((3 * rank, n), BF16)],
        ),
        out_shape=(jax.ShapeDtypeStruct((rows, n), F32), jax.ShapeDtypeStruct((n, rank), F32)),
    )(half, left, own, other, squares, near_core(weight))


class Axis:
    def __init__(self, mesh, name):
        self.name, self.size = name, mesh.shape[name]
        self.bits = self.size.bit_length() - 1

    def swap(self, value, bit):
        return lax.ppermute(value, self.name, [(i, i ^ (1 << bit)) for i in range(self.size)])

    def place(self, bit):
        return (lax.axis_index(self.name) >> bit) & 1

    def exchange(self, value, bit):
        return value + self.swap(value, bit)

    def scatter(self, value, bit, dim=0):
        half = value.shape[dim] // 2
        here = self.place(bit)
        keep = lax.dynamic_slice_in_dim(value, here * half, half, dim)
        return keep + self.swap(lax.dynamic_slice_in_dim(value, (1 - here) * half, half, dim), bit)

    def gather(self, value, bit):
        other = self.swap(value, bit)
        first = jnp.concatenate([value, other])
        return jnp.where(self.place(bit) == 0, first, jnp.concatenate([other, value]))

    def total(self, value, bits):
        for bit in bits[:-1]:
            value = self.scatter(value, bit)
        value = self.exchange(value, bits[-1])
        for bit in bits[-2::-1]:
            value = self.gather(value, bit)
        return value


def on_device(col, row, weight, momentum, gradient, right_factor):
    rows, n = momentum.shape
    count = n * col.size
    near = col.bits // 2
    order = tuple(range(col.bits))
    orders = (order, order[near:] + order[:near] if near == 0 else (near,) + tuple(b for b in order if b != near))
    parts = 4
    size = rows // parts
    lefts, combined, cross, gram, right = [], [], None, None, right_factor
    for part in range(parts):
        got = left_part(momentum, gradient, right, part == 0, part * size, size)
        right = got[2] if part == 0 else right
        combined.append(got[1])
        lefts.append(col.total(got[0], orders[part % 2]))
    for part in range(parts - 1):
        gram = gram_part(lefts[part], gram)
        cross = cross_part(lefts[part], combined[part], cross)
    gram = row.exchange(gram_part(lefts[-1], gram), 0)
    for bit in range(1, row.bits - 1):
        gram = row.exchange(gram, bit)
    last, gram = lax.optimization_barrier((lefts[-1], gram))
    other = row.swap(gram, row.bits - 1)
    cross = cross_part(last, combined[-1], cross)
    gram = gram + other
    half = row.place(0).astype(jnp.int32).reshape(1)
    cross = row.scatter(cross, 0, 1)
    for bit in range(1, row.bits - 1):
        cross = row.exchange(cross, bit)
    other = row.swap(cross, row.bits - 1)
    gram, _ = lax.optimization_barrier((gram, cross))
    inverse = inverse_factor(gram)
    left = basis(jnp.concatenate(lefts), inverse)
    own, squares = right_side(inverse, cross + other)
    other = row.swap(own, 0)
    squares = row.exchange(squares, 0)
    pieces = [(half, own, 0, parts), (1 - half, other, 0, parts // 2), (1 - half, other, parts // 2, parts)]
    new_momentum = None
    for bit in range(col.bits):
        squares = col.exchange(squares, bit)
        if bit < len(pieces):
            side, value, start, stop = pieces[bit]
            new_momentum = momentum_half(side, left, value, combined[start:stop], start, new_momentum)
    new_weight, new_factor = weight_update(half, left, own, other, squares, weight, count)
    return new_weight, new_momentum, new_factor


def solution(mesh):
    col, row = Axis(mesh, "col"), Axis(mesh, "row")

    def body(*args):
        return on_device(col, row, *args)

    in_specs = (P("row", "col"), P("row", "col"), P("row", "col"), P("col", None))
    out_specs = (P("row", "col"), P("row", "col"), P("col", None))
    return jax.shard_map(body, mesh=mesh, in_specs=in_specs, out_specs=out_specs, check_vma=False)
```

time: 424 us -> 202 us (0.48); the launches traced: 418 us -> 201 us
  matrix products: 127 us -> 0 us
  waiting for transfers between devices: 188 us -> 66.1 us
  Pallas kernels: 0 us -> 85.6 us
  other arithmetic: 56.8 us -> 5.38 us
  starting transfers between devices: 0.65 us -> 34.7 us
  blocking collectives: 21.3 us -> 0 us
  between operations: 15.7 us -> 1.18 us
    psum x3 -> x0, waiting for transfers between devices: 188 us -> none  [the longest x1 105 us: on_device(): left_raw = lax.psum(partial_value, 'col')]
    dot_general x5 -> x0, matrix products: 122 us -> none  [contract(): lax.dot_general(first, second, (((first_dim,), (second_dim,)), ((), ())),...]
    pallas_call x0 -> x19, Pallas kernels: none -> 85.6 us  [the longest x1 27.5 us: inverse_factor(): call(inverse_kernel, 12 * rank ** 3 * 20, rank * rank * 8, out_shape=jax....]
    ppermute x0 -> x29, waiting for transfers between devices: none -> 66.1 us  [swap(): lax.ppermute(value, self.name, [(i, i ^ 1 << bit) for i in range(self.siz...]
    another operation x9 -> x0, other arithmetic: 53.7 us -> none  [the longest x6 34 us: orthonormal(): lower = jnp.linalg.cholesky(gram_matrix)]
    ppermute x0 -> x29, starting transfers between devices: none -> 34.7 us  [swap(): lax.ppermute(value, self.name, [(i, i ^ 1 << bit) for i in range(self.siz...]
    psum x1 -> x0, blocking collectives: 21.3 us -> none  [on_device(): squares = lax.psum(jnp.sum(right_raw * right_raw, axis=0), 'col')]
    add x0 -> x20, other arithmetic: none -> 5 us  [the longest x9 4.62 us: scatter(): keep + self.swap(lax.dynamic_slice_in_dim(value, (1 - here) * half, half,...]
  transfers between devices with their start and end apart: 3 -> 29, of which waited for: 3 -> 14; matrix products, arithmetic and copies ran while one was open for 0% -> 3% of each run, Pallas kernels for 0% -> 29%
where the time goes in v1:
time: 202 us; the launch traced here: 201 us
  Pallas kernels  85.6 us (42%)
  waiting for transfers between devices  66.1 us (33%)
  starting transfers between devices  34.7 us (17%)
  local copies, waits for them, and re-layouts  8.39 us (4%)
  other arithmetic  5.38 us (3%)
    ppermute x29, waiting for transfers between devices, swap(): lax.ppermute(value, self.name, [(i, i ^ 1 << bit) for i in range(self.siz...  66.1 us
    ppermute x29, starting transfers between devices, swap(): lax.ppermute(value, self.name, [(i, i ^ 1 << bit) for i in range(self.siz...  34.7 us
    pallas_call x1, Pallas kernels, inverse_factor(): call(inverse_kernel, 12 * rank ** 3 * 20, rank * rank * 8, out_shape=jax....  27.5 us
    pallas_call x4, Pallas kernels, left_part(): call(functools.partial(left_kernel, opening), 6 * rows * n * rank, rows *...  19.9 us
    pallas_call x3, Pallas kernels, momentum_half(): pl.pallas_call(functools.partial(momentum_kernel, len(parts)), name='mome...  13 us
    pallas_call x1, Pallas kernels, weight_update(): pl.pallas_call(functools.partial(weight_kernel, float(count)), name='weig...  11.4 us
    pallas_call x4, Pallas kernels, cross_part(): call(cross_kernel, 6 * rows * n * rank, rank * n * 8, in_specs=[RESIDENT]...  7.97 us
    unnamed x44, local copies, waits for them, and re-layouts  4.8 us
  transfers between devices with their start and end apart: 29, of which 14 were waited for; matrix products, arithmetic and copies ran while one was open for 3% of the time, Pallas kernels for 29%

profile of v1, /device:TPU:0, one launch (start us, length us, event | category | flops | bytes accessed | tf_op | source)
XLA Modules:
  0.0 201.4 jit_solution(4970597291629428577)
XLA Ops:
  0.6 5.7 %shard_map.67 = (f32[512,256]{1,0:T(8,128)S(1)}, f32[512,2048]{1,0:T(8,128)}, bf16[6144,256]{1,0:T(8,128)(2,1)S(1)}) custom-call(f32[2048,2048]{1,0:T(8,128)} %m_ref.7, bf16[2048,2048]{1,0:T(8,128)(2,1)} %g_ref.7, f32[2048,256]{1,0:T(8,128)} %r_ref.1), custom_call_target="tpu_custom_call" | custom-call | flops 1610612736 | bytes 6291456 | tf_op jit(solution)/shard_map/pallas_call | solution.py:94
  7.2 3.0 %collective-permute-start = (f32[256,256]{1,0:T(8,128)S(1)}, f32[256,256]{1,0:T(8,128)}, u32[]{:S(2)}, u32[]{:S(2)}) collective-permute-start(f32[256,256]{1,0:T(8,128)S(1)} %constant_dynamic-slice_fusion.8), channel_id=1, source_target_pairs={{0,4},{4,0},{8,12},{12,8},{16,20},{20,16},{24,28},{28,24},{1,5},{5... | collective-permute-start | bytes 786440 | tf_op jit(solution)/shard_map/ppermute | solution.py:300
  10.2 4.7 %shard_map.70 = (f32[512,256]{1,0:T(8,128)S(1)}, f32[512,2048]{1,0:T(8,128)}) custom-call(f32[2048,2048]{1,0:T(8,128)} %m_ref.7, bf16[2048,2048]{1,0:T(8,128)(2,1)} %g_ref.7, bf16[6144,256]{1,0:T(8,128)(2,1)S(1)} %get-tuple-element.20.r_ref), custom_call_target="tpu_custom_call" | custom-call | flops 1610612736 | bytes 6291456 | tf_op jit(solution)/shard_map/pallas_call | solution.py:94
  15.7 1.7 constant_dynamic-slice_fusion.2
  18.9 4.7 %shard_map.69 = (f32[512,256]{1,0:T(8,128)S(1)}, f32[512,2048]{1,0:T(8,128)}) custom-call(f32[2048,2048]{1,0:T(8,128)} %m_ref.7, bf16[2048,2048]{1,0:T(8,128)(2,1)} %g_ref.7, bf16[6144,256]{1,0:T(8,128)(2,1)S(1)} %get-tuple-element.20.r_ref), custom_call_target="tpu_custom_call" | custom-call | flops 1610612736 | bytes 6291456 | tf_op jit(solution)/shard_map/pallas_call | solution.py:94
  25.1 4.7 %shard_map.68 = (f32[512,256]{1,0:T(8,128)S(1)}, f32[512,2048]{1,0:T(8,128)}) custom-call(f32[2048,2048]{1,0:T(8,128)} %m_ref.7, bf16[2048,2048]{1,0:T(8,128)(2,1)} %g_ref.7, bf16[6144,256]{1,0:T(8,128)(2,1)S(1)} %get-tuple-element.20.r_ref), custom_call_target="tpu_custom_call" | custom-call | flops 1610612736 | bytes 6291456 | tf_op jit(solution)/shard_map/pallas_call | solution.py:94
  31.9 2.0 collective-permute-start.1
  38.1 1.8 collective-permute-done.5
  42.2 3.2 %collective-permute-start.2 = (f32[128,256]{1,0:T(8,128)S(1)}, f32[128,256]{1,0:T(8,128)S(1)}, u32[]{:S(2)}, u32[]{:S(2)}) collective-permute-start(f32[128,256]{1,0:T(8,128)S(1)} %dynamic-slice_add_fusion.8), channel_id=1, source_target_pairs={{0,16},{4,20},{8,24},{12,28},{16,0},{20,4},{24,8},{28,12},{1,17},{... | collective-permute-start | bytes 393224 | tf_op jit(solution)/shard_map/ppermute | solution.py:300
  45.5 3.0 %collective-permute-start.12 = (f32[128,256]{1,0:T(8,128)S(1)}, f32[128,256]{1,0:T(8,128)S(1)}, u32[]{:S(2)}, u32[]{:S(2)}) collective-permute-start(f32[128,256]{1,0:T(8,128)S(1)} %dynamic-slice_add_fusion.6), channel_id=1, source_target_pairs={{0,16},{4,20},{8,24},{12,28},{16,0},{20,4},{24,8},{28,12},{1,17},{... | collective-permute-start | bytes 393224 | tf_op jit(solution)/shard_map/ppermute | solution.py:300
  48.6 10.8 %collective-permute-done.2 = f32[128,256]{1,0:T(8,128)S(1)} collective-permute-done((f32[128,256]{1,0:T(8,128)S(1)}, f32[128,256]{1,0:T(8,128)S(1)}, u32[]{:S(2)}, u32[]{:S(2)}) %collective-permute-start.2) | collective-permute-done | bytes 131104 | tf_op jit(solution)/shard_map/ppermute | solution.py:300
  59.5 4.5 %collective-permute-done.12 = f32[128,256]{1,0:T(8,128)S(1)} collective-permute-done((f32[128,256]{1,0:T(8,128)S(1)}, f32[128,256]{1,0:T(8,128)S(1)}, u32[]{:S(2)}, u32[]{:S(2)}) %collective-permute-start.12) | collective-permute-done | bytes 131104 | tf_op jit(solution)/shard_map/ppermute | solution.py:300
  72.2 3.3 %collective-permute-start.9 = (f32[256,256]{1,0:T(8,128)S(1)}, f32[256,256]{1,0:T(8,128)S(1)}, u32[]{:S(2)}, u32[]{:S(2)}) collective-permute-start(f32[256,256]{1,0:T(8,128)S(1)} %maximum_select_fusion.5), channel_id=1, source_target_pairs={{0,8},{4,12},{8,0},{12,4},{16,24},{20,28},{24,16},{28,20},{1,9},{5... | collective-permute-start | bytes 786440 | tf_op jit(solution)/shard_map/ppermute | solution.py:300
  75.6 2.2 %collective-permute-done.4 = f32[256,256]{1,0:T(8,128)S(1)} collective-permute-done((f32[256,256]{1,0:T(8,128)S(1)}, f32[256,256]{1,0:T(8,128)S(1)}, u32[]{:S(2)}, u32[]{:S(2)}) %collective-permute-start.4) | collective-permute-done | bytes 262176 | tf_op jit(solution)/shard_map/ppermute | solution.py:300
  77.8 4.0 %collective-permute-done.14 = f32[256,256]{1,0:T(8,128)S(1)} collective-permute-done((f32[256,256]{1,0:T(8,128)S(1)}, f32[256,256]{1,0:T(8,128)S(1)}, u32[]{:S(2)}, u32[]{:S(2)}) %collective-permute-start.14) | collective-permute-done | bytes 262176 | tf_op jit(solution)/shard_map/ppermute | solution.py:300
  84.1 1.9 shard_map.75.refs_0_
  86.8 2.0 %shard_map.76.refs_0_ = f32[256,2048]{1,0:T(8,128)S(1)} custom-call(f32[512,256]{1,0:T(8,128)S(1)} %maximum_select_fusion.1.refs_0_.l_ref, f32[512,2048]{1,0:T(8,128)S(1)} %copy-done.4, f32[256,2048]{1,0:T(8,128)S(1)} %shard_map.75.refs_0_), custom_call_target="tpu_custom_call", output_to_operand_aliasing={{}: (2, {})} | custom-call | flops 1610612736 | bytes 4194304 | tf_op jit(solution)/shard_map/pallas_call | solution.py:117
  89.0 2.0 %shard_map.77.refs_0_ = f32[256,2048]{1,0:T(8,128)S(1)} custom-call(f32[512,256]{1,0:T(8,128)S(1)} %maximum_select_fusion.2.refs_0_.l_ref, f32[512,2048]{1,0:T(8,128)S(1)} %copy-done.2, f32[256,2048]{1,0:T(8,128)S(1)} %shard_map.76.refs_0_), custom_call_target="tpu_custom_call", output_to_operand_aliasing={{}: (2, {})} | custom-call | flops 1610612736 | bytes 4194304 | tf_op jit(solution)/shard_map/pallas_call | solution.py:117
  91.2 2.0 %shard_map.78 = f32[256,2048]{1,0:T(8,128)S(1)} custom-call(f32[512,256]{1,0:T(8,128)S(1)} %maximum_select_fusion.3.refs_0_.l_ref, f32[512,2048]{1,0:T(8,128)S(1)} %copy-done, f32[256,2048]{1,0:T(8,128)S(1)} %shard_map.77.refs_0_), custom_call_target="tpu_custom_call", output_to_operand_aliasing={{}: (2, {})} | custom-call | flops 1610612736 | bytes 4194304 | tf_op jit(solution)/shard_map/pallas_call | solution.py:117
  94.8 2.6 %collective-permute-done.22 = f32[256,1024]{1,0:T(8,128)} collective-permute-done((f32[256,1024]{1,0:T(8,128)}, f32[256,1024]{1,0:T(8,128)}, u32[]{:S(2)}, u32[]{:S(2)}) %collective-permute-start.22) | collective-permute-done | bytes 1048608 | tf_op jit(solution)/shard_map/ppermute | solution.py:300
  100.9 29.0 %collective-permute-done.21 = f32[256,256]{1,0:T(8,128)S(1)} collective-permute-done((f32[256,256]{1,0:T(8,128)S(1)}, f32[256,256]{1,0:T(8,128)S(1)}, u32[]{:S(2)}, u32[]{:S(2)}) %collective-permute-start.21) | collective-permute-done | bytes 262176 | tf_op jit(solution)/shard_map/ppermute | solution.py:300
  130.0 27.5 %shard_map.79.x_ref = f32[256,256]{1,0:T(8,128)S(1)} custom-call(f32[256,256]{1,0:T(8,128)S(1)} %add.119.g_ref), custom_call_target="tpu_custom_call" | custom-call | flops 4026531840 | bytes 524288 | tf_op jit(solution)/shard_map/pallas_call | solution.py:172
  159.4 2.3 %collective-permute-done.25 = f32[256,128]{1,0:T(8,128)S(1)} collective-permute-done((f32[256,128]{1,0:T(8,128)S(1)}, f32[256,128]{1,0:T(8,128)S(1)}, u32[]{:S(2)}, u32[]{:S(2)}) %collective-permute-start.25) | collective-permute-done | bytes 131104 | tf_op jit(solution)/shard_map/ppermute | solution.py:300
  163.5 3.9 %collective-permute-done.26 = f32[256,128]{1,0:T(8,128)S(1)} collective-permute-done((f32[256,128]{1,0:T(8,128)S(1)}, f32[256,128]{1,0:T(8,128)S(1)}, u32[]{:S(2)}, u32[]{:S(2)}) %collective-permute-start.26) | collective-permute-done | bytes 131104 | tf_op jit(solution)/shard_map/ppermute | solution.py:300
  168.3 1.8 shard_map.80.l_ref
  170.2 2.3 %collective-permute-done.27 = f32[256,128]{1,0:T(8,128)S(1)} collective-permute-done((f32[256,128]{1,0:T(8,128)S(1)}, f32[256,128]{1,0:T(8,128)S(1)}, u32[]{:S(2)}, u32[]{:S(2)}) %collective-permute-start.27) | collective-permute-done | bytes 131104 | tf_op jit(solution)/shard_map/ppermute | solution.py:300
  172.5 2.4 %collective-permute-start.28 = (f32[256,128]{1,0:T(8,128)S(1)}, f32[256,128]{1,0:T(8,128)S(1)}, u32[]{:S(2)}, u32[]{:S(2)}) collective-permute-start(f32[256,128]{1,0:T(8,128)S(1)} %add.126), channel_id=1, source_target_pairs={{0,16},{4,20},{8,24},{12,28},{16,0},{20,4},{24,8},{28,12},{1,17},{... | collective-permute-start | bytes 393224 | tf_op jit(solution)/shard_map/ppermute | solution.py:300
  174.9 5.9 %momentum.3.refs_2_ = f32[2048,2048]{1,0:T(8,128)} custom-call(s32[1]{0:T(128)} %bitcast.half_ref, f32[2048,256]{1,0:T(8,128)S(1)} %shard_map.80.l_ref, f32[256,1024]{1,0:T(8,128)S(1)} %get-tuple-element.31.a_ref.r_ref, f32[512,2048]{1,0:T(8,128)S(1)} %copy-done.7, f32[512,2048]{1,0:T(8,128)S(1)} %copy-done.5, f32[512,2048]{1,0:T(8,128)S(1)} %copy-done.3, ...), custom_call_target="tpu_custom_call" | custom-call | flops 2147483648 | bytes 8388608 | tf_op jit(solution)/shard_map/momentum/pallas_call | solution.py:231
  180.9 3.6 %momentum.4.refs_2_ = f32[2048,2048]{1,0:T(8,128)} custom-call(s32[1]{0:T(128)S(6)} %sub.22.half_ref, f32[2048,256]{1,0:T(8,128)S(1)} %shard_map.80.l_ref, f32[256,1024]{1,0:T(8,128)S(1)} %collective-permute-done.24.b_ref.r_ref, f32[512,2048]{1,0:T(8,128)S(1)} %copy-done.7, f32[512,2048]{1,0:T(8,128)S(1)} %copy-done.5, ...), custom_call_target="tpu_custom_call", output_to_operand_aliasing={{}: (5, {})} | custom-call | flops 1073741824 | bytes 4194304 | tf_op jit(solution)/shard_map/momentum/pallas_call | solution.py:231
  184.5 3.5 %momentum.5 = f32[2048,2048]{1,0:T(8,128)} custom-call(s32[1]{0:T(128)S(6)} %sub.22.half_ref, f32[2048,256]{1,0:T(8,128)S(1)} %shard_map.80.l_ref, f32[256,1024]{1,0:T(8,128)S(1)} %collective-permute-done.24.b_ref.r_ref, f32[512,2048]{1,0:T(8,128)S(1)} %copy-done.3, f32[512,2048]{1,0:T(8,128)S(1)} %copy-done.1, ...), custom_call_target="tpu_custom_call", output_to_operand_aliasing={{}: (5, {})} | custom-call | flops 1073741824 | bytes 4194304 | tf_op jit(solution)/shard_map/momentum/pallas_call | solution.py:231
  188.0 1.9 slice-done.3
  189.9 11.4 %weight.1 = (f32[2048,2048]{1,0:T(8,128)}, f32[2048,256]{1,0:T(8,128)}) custom-call(s32[1]{0:T(128)} %bitcast.half_ref, f32[2048,256]{1,0:T(8,128)S(1)} %shard_map.80.l_ref, f32[256,1024]{1,0:T(8,128)S(1)} %get-tuple-element.31.a_ref.r_ref, f32[256,1024]{1,0:T(8,128)S(1)} %collective-permute-done.24.b_ref.r_ref, f32[256,128]{1,0:T(8,128)S(1)} %add.127.s_ref, ...), custom_call_target="tpu_custom_call" | custom-call | flops 6442450944 | bytes 33554432 | tf_op jit(solution)/shard_map/weight/pallas_call | solution.py:272
  (128 shorter events, 34.5 us)
Async XLA Ops:
  7.2 23.6 %collective-permute-start = (f32[256,256]{1,0:T(8,128)S(1)}, f32[256,256]{1,0:T(8,128)}, u32[]{:S(2)}, u32[]{:S(2)}) collective-permute-start(f32[256,256]{1,0:T(8,128)S(1)} %constant_dynamic-slice_fusion.8), channel_id=1, source_target_pairs={{0,4},{4,0},{8,12},{12,8},{16,20},{20,16},{24,28},{28,24},{1,5},{5... | collective-permute-start | bytes 786440 | tf_op jit(solution)/shard_map/ppermute | solution.py:300
  17.4 16.6 %collective-permute-start.15 = (f32[256,256]{1,0:T(8,128)}, f32[256,256]{1,0:T(8,128)}, u32[]{:S(2)}, u32[]{:S(2)}) collective-permute-start(f32[256,256]{1,0:T(8,128)} %constant_dynamic-slice_fusion.2), channel_id=1, source_target_pairs={{0,8},{4,12},{8,0},{12,4},{16,24},{20,28},{24,16},{28,20},{1,9},{5... | collective-permute-start | bytes 786440 | tf_op jit(solution)/shard_map/ppermute | solution.py:300
  24.5 12.0 %collective-permute-start.10 = (f32[256,256]{1,0:T(8,128)}, f32[256,256]{1,0:T(8,128)}, u32[]{:S(2)}, u32[]{:S(2)}) collective-permute-start(f32[256,256]{1,0:T(8,128)} %constant_dynamic-slice_fusion.4), channel_id=1, source_target_pairs={{0,4},{4,0},{8,12},{12,8},{16,20},{20,16},{24,28},{28,24},{1,5},{5... | collective-permute-start | bytes 786440 | tf_op jit(solution)/shard_map/ppermute | solution.py:300
  30.7 9.2 %collective-permute-start.5 = (f32[256,256]{1,0:T(8,128)S(1)}, f32[256,256]{1,0:T(8,128)S(1)}, u32[]{:S(2)}, u32[]{:S(2)}) collective-permute-start(f32[256,256]{1,0:T(8,128)S(1)} %constant_dynamic-slice_fusion.6), channel_id=1, source_target_pairs={{0,8},{4,12},{8,0},{12,4},{16,24},{20,28},{24,16},{28,20},{1,9},{5... | collective-permute-start | bytes 786440 | tf_op jit(solution)/shard_map/ppermute | solution.py:300
  31.9 10.2 %collective-permute-start.1 = (f32[128,256]{1,0:T(8,128)S(1)}, f32[128,256]{1,0:T(8,128)S(1)}, u32[]{:S(2)}, u32[]{:S(2)}) collective-permute-start(f32[128,256]{1,0:T(8,128)S(1)} %constant_dynamic-slice_fusion.7), channel_id=1, source_target_pairs={{0,8},{4,12},{8,0},{12,4},{16,24},{20,28},{24,16},{28,20},{1,9},{5... | collective-permute-start | bytes 393224 | tf_op jit(solution)/shard_map/ppermute | solution.py:300
  35.0 10.4 %collective-permute-start.16 = (f32[128,256]{1,0:T(8,128)S(1)}, f32[128,256]{1,0:T(8,128)S(1)}, u32[]{:S(2)}, u32[]{:S(2)}) collective-permute-start(f32[128,256]{1,0:T(8,128)S(1)} %constant_dynamic-slice_fusion.1), channel_id=1, source_target_pairs={{0,4},{4,0},{8,12},{12,8},{16,20},{20,16},{24,28},{28,24},{1,5},{5... | collective-permute-start | bytes 393224 | tf_op jit(solution)/shard_map/ppermute | solution.py:300
  37.6 7.9 %collective-permute-start.11 = (f32[128,256]{1,0:T(8,128)S(1)}, f32[128,256]{1,0:T(8,128)S(1)}, u32[]{:S(2)}, u32[]{:S(2)}) collective-permute-start(f32[128,256]{1,0:T(8,128)S(1)} %constant_dynamic-slice_fusion.3), channel_id=1, source_target_pairs={{0,8},{4,12},{8,0},{12,4},{16,24},{20,28},{24,16},{28,20},{1,9},{5... | collective-permute-start | bytes 393224 | tf_op jit(solution)/shard_map/ppermute | solution.py:300
  40.0 8.5 %collective-permute-start.6 = (f32[128,256]{1,0:T(8,128)S(1)}, f32[128,256]{1,0:T(8,128)S(1)}, u32[]{:S(2)}, u32[]{:S(2)}) collective-permute-start(f32[128,256]{1,0:T(8,128)S(1)} %constant_dynamic-slice_fusion.5), channel_id=1, source_target_pairs={{0,4},{4,0},{8,12},{12,8},{16,20},{20,16},{24,28},{28,24},{1,5},{5... | collective-permute-start | bytes 393224 | tf_op jit(solution)/shard_map/ppermute | solution.py:300
  42.2 17.2 %collective-permute-start.2 = (f32[128,256]{1,0:T(8,128)S(1)}, f32[128,256]{1,0:T(8,128)S(1)}, u32[]{:S(2)}, u32[]{:S(2)}) collective-permute-start(f32[128,256]{1,0:T(8,128)S(1)} %dynamic-slice_add_fusion.8), channel_id=1, source_target_pairs={{0,16},{4,20},{8,24},{12,28},{16,0},{20,4},{24,8},{28,12},{1,17},{... | collective-permute-start | bytes 393224 | tf_op jit(solution)/shard_map/ppermute | solution.py:300
  45.4 18.7 %collective-permute-start.17 = (f32[128,256]{1,0:T(8,128)S(1)}, f32[128,256]{1,0:T(8,128)S(1)}, u32[]{:S(2)}, u32[]{:S(2)}) collective-permute-start(f32[128,256]{1,0:T(8,128)S(1)} %dynamic-slice_add_fusion.5), channel_id=1, source_target_pairs={{0,16},{4,20},{8,24},{12,28},{16,0},{20,4},{24,8},{28,12},{1,17},{... | collective-permute-start | bytes 393224 | tf_op jit(solution)/shard_map/ppermute | solution.py:300
  45.5 18.5 %collective-permute-start.12 = (f32[128,256]{1,0:T(8,128)S(1)}, f32[128,256]{1,0:T(8,128)S(1)}, u32[]{:S(2)}, u32[]{:S(2)}) collective-permute-start(f32[128,256]{1,0:T(8,128)S(1)} %dynamic-slice_add_fusion.6), channel_id=1, source_target_pairs={{0,16},{4,20},{8,24},{12,28},{16,0},{20,4},{24,8},{28,12},{1,17},{... | collective-permute-start | bytes 393224 | tf_op jit(solution)/shard_map/ppermute | solution.py:300
  48.5 17.2 %collective-permute-start.7 = (f32[128,256]{1,0:T(8,128)S(1)}, f32[128,256]{1,0:T(8,128)S(1)}, u32[]{:S(2)}, u32[]{:S(2)}) collective-permute-start(f32[128,256]{1,0:T(8,128)S(1)} %dynamic-slice_add_fusion.7), channel_id=1, source_target_pairs={{0,16},{4,20},{8,24},{12,28},{16,0},{20,4},{24,8},{28,12},{1,17},{... | collective-permute-start | bytes 393224 | tf_op jit(solution)/shard_map/ppermute | solution.py:300
  59.4 8.8 %collective-permute-start.3 = (f32[128,256]{1,0:T(8,128)S(1)}, f32[128,256]{1,0:T(8,128)S(1)}, u32[]{:S(2)}, u32[]{:S(2)}) collective-permute-start(f32[128,256]{1,0:T(8,128)S(1)} %add.104), channel_id=1, source_target_pairs={{0,8},{4,12},{8,0},{12,4},{16,24},{20,28},{24,16},{28,20},{1,9},{5... | collective-permute-start | bytes 393224 | tf_op jit(solution)/shard_map/ppermute | solution.py:300
  64.0 6.0 %collective-permute-start.13 = (f32[128,256]{1,0:T(8,128)S(1)}, f32[128,256]{1,0:T(8,128)S(1)}, u32[]{:S(2)}, u32[]{:S(2)}) collective-permute-start(f32[128,256]{1,0:T(8,128)S(1)} %add.114), channel_id=1, source_target_pairs={{0,8},{4,12},{8,0},{12,4},{16,24},{20,28},{24,16},{28,20},{1,9},{5... | collective-permute-start | bytes 393224 | tf_op jit(solution)/shard_map/ppermute | solution.py:300
  64.1 11.3 %collective-permute-start.18 = (f32[128,256]{1,0:T(8,128)S(1)}, f32[128,256]{1,0:T(8,128)S(1)}, u32[]{:S(2)}, u32[]{:S(2)}) collective-permute-start(f32[128,256]{1,0:T(8,128)S(1)} %add.117), channel_id=1, source_target_pairs={{0,4},{4,0},{8,12},{12,8},{16,20},{20,16},{24,28},{28,24},{1,5},{5... | collective-permute-start | bytes 393224 | tf_op jit(solution)/shard_map/ppermute | solution.py:300
  65.7 6.4 %collective-permute-start.8 = (f32[128,256]{1,0:T(8,128)S(1)}, f32[128,256]{1,0:T(8,128)S(1)}, u32[]{:S(2)}, u32[]{:S(2)}) collective-permute-start(f32[128,256]{1,0:T(8,128)S(1)} %add.111), channel_id=1, source_target_pairs={{0,4},{4,0},{8,12},{12,8},{16,20},{20,16},{24,28},{28,24},{1,5},{5... | collective-permute-start | bytes 393224 | tf_op jit(solution)/shard_map/ppermute | solution.py:300
  68.2 9.5 %collective-permute-start.4 = (f32[256,256]{1,0:T(8,128)S(1)}, f32[256,256]{1,0:T(8,128)S(1)}, u32[]{:S(2)}, u32[]{:S(2)}) collective-permute-start(f32[256,256]{1,0:T(8,128)S(1)} %maximum_select_fusion.4), channel_id=1, source_target_pairs={{0,4},{4,0},{8,12},{12,8},{16,20},{20,16},{24,28},{28,24},{1,5},{5... | collective-permute-start | bytes 786440 | tf_op jit(solution)/shard_map/ppermute | solution.py:300
  70.1 11.7 %collective-permute-start.14 = (f32[256,256]{1,0:T(8,128)S(1)}, f32[256,256]{1,0:T(8,128)S(1)}, u32[]{:S(2)}, u32[]{:S(2)}) collective-permute-start(f32[256,256]{1,0:T(8,128)S(1)} %maximum_select_fusion.6), channel_id=1, source_target_pairs={{0,4},{4,0},{8,12},{12,8},{16,20},{20,16},{24,28},{28,24},{1,5},{5... | collective-permute-start | bytes 786440 | tf_op jit(solution)/shard_map/ppermute | solution.py:300
  72.2 9.7 %collective-permute-start.9 = (f32[256,256]{1,0:T(8,128)S(1)}, f32[256,256]{1,0:T(8,128)S(1)}, u32[]{:S(2)}, u32[]{:S(2)}) collective-permute-start(f32[256,256]{1,0:T(8,128)S(1)} %maximum_select_fusion.5), channel_id=1, source_target_pairs={{0,8},{4,12},{8,0},{12,4},{16,24},{20,28},{24,16},{28,20},{1,9},{5... | collective-permute-start | bytes 786440 | tf_op jit(solution)/shard_map/ppermute | solution.py:300
  75.5 10.5 %collective-permute-start.19 = (f32[256,256]{1,0:T(8,128)S(1)}, f32[256,256]{1,0:T(8,128)S(1)}, u32[]{:S(2)}, u32[]{:S(2)}) collective-permute-start(f32[256,256]{1,0:T(8,128)S(1)} %maximum_select_fusion.7), channel_id=1, source_target_pairs={{0,8},{4,12},{8,0},{12,4},{16,24},{20,28},{24,16},{28,20},{1,9},{5... | collective-permute-start | bytes 786440 | tf_op jit(solution)/shard_map/ppermute | solution.py:300
  86.7 4.3 %collective-permute-start.20 = (f32[256,256]{1,0:T(8,128)S(1)}, f32[256,256]{1,0:T(8,128)S(1)}, u32[]{:S(2)}, u32[]{:S(2)}) collective-permute-start(f32[256,256]{1,0:T(8,128)S(1)} %shard_map.74), channel_id=1, source_target_pairs={{0,1},{1,0},{2,3},{3,2},{4,5},{5,4},{6,7},{7,6},{8,9},{9,8},{10,11... | collective-permute-start | bytes 786440 | tf_op jit(solution)/shard_map/ppermute | solution.py:300
  94.3 3.1 %collective-permute-start.22 = (f32[256,1024]{1,0:T(8,128)}, f32[256,1024]{1,0:T(8,128)}, u32[]{:S(2)}, u32[]{:S(2)}) collective-permute-start(f32[256,1024]{1,0:T(8,128)} %constant_dynamic-slice_fusion), channel_id=1, source_target_pairs={{0,1},{1,0},{2,3},{3,2},{4,5},{5,4},{6,7},{7,6},{8,9},{9,8},{10,11... | collective-permute-start | bytes 3145736 | tf_op jit(solution)/shard_map/ppermute | solution.py:300
  98.8 58.7 %collective-permute-start.23 = (f32[256,1024]{1,0:T(8,128)S(1)}, f32[256,1024]{1,0:T(8,128)S(1)}, u32[]{:S(2)}, u32[]{:S(2)}) collective-permute-start(f32[256,1024]{1,0:T(8,128)S(1)} %dynamic-slice_add_fusion), channel_id=1, source_target_pairs={{0,2},{1,3},{2,0},{3,1},{4,6},{5,7},{6,4},{7,5},{8,10},{9,11},{10,... | collective-permute-start | bytes 3145736 | tf_op jit(solution)/shard_map/ppermute | solution.py:300
  100.4 29.5 %collective-permute-start.21 = (f32[256,256]{1,0:T(8,128)S(1)}, f32[256,256]{1,0:T(8,128)S(1)}, u32[]{:S(2)}, u32[]{:S(2)}) collective-permute-start(f32[256,256]{1,0:T(8,128)S(1)} %add.118), channel_id=1, source_target_pairs={{0,2},{1,3},{2,0},{3,1},{4,6},{5,7},{6,4},{7,5},{8,10},{9,11},{10,... | collective-permute-start | bytes 786440 | tf_op jit(solution)/shard_map/ppermute | solution.py:300
  130.0 33.4 %copy-start.11 = (f32[512,256]{1,0:T(8,128)S(1)}, f32[512,256]{1,0:T(8,128)}, u32[]{:S(2)}) copy-start(f32[512,256]{1,0:T(8,128)} %copy-done.10) | copy-start | bytes 1572868
  157.5 17.3 %copy-start.7 = (f32[512,2048]{1,0:T(8,128)S(1)}, f32[512,2048]{1,0:T(8,128)}, u32[]{:S(2)}) copy-start(f32[512,2048]{1,0:T(8,128)} %get-tuple-element.29.c_ref.refs_0_) | copy-start | bytes 12582916
  157.7 17.2 %copy-start.5 = (f32[512,2048]{1,0:T(8,128)S(1)}, f32[512,2048]{1,0:T(8,128)}, u32[]{:S(2)}) copy-start(f32[512,2048]{1,0:T(8,128)} %get-tuple-element.28.c_ref.refs_1_) | copy-start | bytes 12582916
  158.9 22.0 %collective-permute-start.24 = (f32[256,1024]{1,0:T(8,128)S(1)}, f32[256,1024]{1,0:T(8,128)S(1)}, u32[]{:S(2)}, u32[]{:S(2)}) collective-permute-start(f32[256,1024]{1,0:T(8,128)S(1)} %get-tuple-element.31.a_ref.r_ref), channel_id=1, source_target_pairs={{0,1},{1,0},{2,3},{3,2},{4,5},{5,4},{6,7},{7,6},{8,9},{9,8},{10,11... | collective-permute-start | bytes 3145736 | tf_op jit(solution)/shard_map/ppermute | solution.py:300
  158.9 2.8 %collective-permute-start.25 = (f32[256,128]{1,0:T(8,128)S(1)}, f32[256,128]{1,0:T(8,128)S(1)}, u32[]{:S(2)}, u32[]{:S(2)}) collective-permute-start(f32[256,128]{1,0:T(8,128)S(1)} %get-tuple-element.32), channel_id=1, source_target_pairs={{0,1},{1,0},{2,3},{3,2},{4,5},{5,4},{6,7},{7,6},{8,9},{9,8},{10,11... | collective-permute-start | bytes 393224 | tf_op jit(solution)/shard_map/ppermute | solution.py:300
  161.8 5.6 %collective-permute-start.26 = (f32[256,128]{1,0:T(8,128)S(1)}, f32[256,128]{1,0:T(8,128)S(1)}, u32[]{:S(2)}, u32[]{:S(2)}) collective-permute-start(f32[256,128]{1,0:T(8,128)S(1)} %add.124), channel_id=1, source_target_pairs={{0,4},{4,0},{8,12},{12,8},{16,20},{20,16},{24,28},{28,24},{1,5},{5... | collective-permute-start | bytes 393224 | tf_op jit(solution)/shard_map/ppermute | solution.py:300
  167.4 5.0 %collective-permute-start.27 = (f32[256,128]{1,0:T(8,128)S(1)}, f32[256,128]{1,0:T(8,128)S(1)}, u32[]{:S(2)}, u32[]{:S(2)}) collective-permute-start(f32[256,128]{1,0:T(8,128)S(1)} %add.125), channel_id=1, source_target_pairs={{0,8},{4,12},{8,0},{12,4},{16,24},{20,28},{24,16},{28,20},{1,9},{5... | collective-permute-start | bytes 393224 | tf_op jit(solution)/shard_map/ppermute | solution.py:300
  172.5 8.3 %collective-permute-start.28 = (f32[256,128]{1,0:T(8,128)S(1)}, f32[256,128]{1,0:T(8,128)S(1)}, u32[]{:S(2)}, u32[]{:S(2)}) collective-permute-start(f32[256,128]{1,0:T(8,128)S(1)} %add.126), channel_id=1, source_target_pairs={{0,16},{4,20},{8,24},{12,28},{16,0},{20,4},{24,8},{28,12},{1,17},{... | collective-permute-start | bytes 393224 | tf_op jit(solution)/shard_map/ppermute | solution.py:300
  (19 other events, 87.9 us)

commit v2 on v1

--- a/solution.py
+++ b/solution.py
@@ -79,7 +79,7 @@
 def left_part(momentum, gradient, right, opening, start, rows):
     n = momentum.shape[1]
     rank = right.shape[1]
-    bm = tile(rows)
+    bm = tile(momentum.shape[0] // sum(SHARES))
     first = start // bm
     block = pl.BlockSpec((bm, n), lambda i: (i + first, 0))
     here = lambda i: (i, 0)
@@ -140,30 +140,31 @@
 
 def inverse_kernel(g_ref, x_ref, work):
     rank = g_ref.shape[0]
-    b = min(32, rank)
+    b = min(128, rank)
     rows = lax.broadcasted_iota(jnp.int32, (rank, rank), 0)
     cols = lax.broadcasted_iota(jnp.int32, (rank, rank), 1)
     work[:, :rank] = g_ref[...]
     work[:, rank:] = jnp.where(rows == cols, 1.0, 0.0).astype(F32)
     r = lax.broadcasted_iota(jnp.int32, (b, b), 0)
     c = lax.broadcasted_iota(jnp.int32, (b, b), 1)
+    sub = lax.broadcasted_iota(jnp.int32, (b, 1), 0)
     for j in range(0, rank, b):
-        block = work[j : j + b, j : j + b]
-        inv = jnp.where(r == c, 1.0, 0.0).astype(F32)
-        aug = jnp.concatenate([block, inv], axis=1)
-        sub = lax.broadcasted_iota(jnp.int32, (b, 2 * b), 0)
-        pivots = jnp.zeros((b, 1), F32)
+        unit = jnp.where(r == c, 1.0, 0.0).astype(F32)
+        both = jnp.concatenate([work[j : j + b, j : j + b], unit], axis=1)
         for i in range(b):
-            pivot = aug[i : i + 1, i : i + 1]
-            row = aug[i : i + 1, :] * (1.0 / pivot)
-            col = jnp.where(sub[:, :1] > i, aug[:, i : i + 1], 0.0)
-            pivots = jnp.where(sub[:, :1] == i, pivot, pivots)
-            aug = aug - col * row
-        inv = aug[:, b:] * lax.rsqrt(pivots)
-        panel = dot(inv, work[j : j + b, :], NN, HIGHEST)
-        work[j : j + b, :] = panel
-        if j + b < rank:
-            work[j + b :, :] -= dot(panel[:, j + b : rank], panel, TN, HIGHEST)
+            top = i // 8 * 8
+            pivot = jnp.broadcast_to(both[i : i + 1, i : i + 1], (1, 2 * b))
+            row = both[i : i + 1, :] * (1.0 / pivot)
+            below = both[top:, :]
+            below = below - jnp.where(sub[top:] > i, below[:, i : i + 1], 0.0) * row
+            both = jnp.concatenate([both[:top], below], axis=0) if top else below
+        pivots = jnp.sum(jnp.where(r == c, both[:, :b], 0.0), axis=1, keepdims=True)
+        inv = both[:, b:] * lax.rsqrt(pivots)
+        done = j + b
+        panel = dot(inv, work[j:done, : rank + done], NN, HIGHEST)
+        work[j:done, : rank + done] = panel
+        if done < rank:
+            work[done:, : rank + done] -= dot(panel[:, done:rank], panel, TN, HIGHEST)
     x_ref[...] = work[:, rank:]
 
 
@@ -202,10 +203,10 @@
     )(inverse, cross)
 
 
-def momentum_kernel(parts, half_ref, l_ref, r_ref, *refs):
+def momentum_kernel(first, half_ref, l_ref, r_ref, m_ref, g_ref, *refs):
     o_ref, split = refs[-2:]
     i = pl.program_id(0)
-    _, width = o_ref.shape
+    bm, width = o_ref.shape
 
     @pl.when(i == 0)
     def _():
@@ -214,38 +215,39 @@
 
     left = l_ref[...].astype(BF16)
     update = dot(jnp.concatenate([left, left], axis=1), split[...], NN)
-    columns = pl.ds(pl.multiple_of(half_ref[0] * width, width), width)
-    for part in range(parts):
-
-        @pl.when(i == part)
-        def _():
-            o_ref[...] = refs[part][:, columns] - 0.05 * update
-
-
-def momentum_half(half, left, right, parts, first, before):
-    rows, rank = left.shape
-    width = right.shape[1]
-    bm = parts[0].shape[0]
+    here = (
+        pl.ds(pl.multiple_of((i + first) * bm, bm), bm),
+        pl.ds(pl.multiple_of(half_ref[0] * width, width), width),
+    )
+    o_ref[...] = (m_ref[here] + g_ref[here].astype(F32)) - 0.05 * update
+
+
+def momentum_half(half, left, right, momentum, gradient, start, stop, before):
+    rows, n = momentum.shape
+    rank, width = right.shape
+    bm = tile((stop - start))
+    first = start // bm
     extra = [] if before is None else [before]
-    n_in = 3 + len(parts) + len(extra)
     return pl.pallas_call(
-        functools.partial(momentum_kernel, len(parts)),
+        functools.partial(momentum_kernel, first),
         name="momentum",
-        cost_estimate=pl.CostEstimate(flops=4 * bm * len(parts) * width * rank, bytes_accessed=bm * len(parts) * width * 4, transcendentals=0),
-        compiler_params=pltpu.CompilerParams(vmem_limit_bytes=16 << 20),
+        cost_estimate=pl.CostEstimate(flops=4 * (stop - start) * width * rank, bytes_accessed=(stop - start) * width * 4, transcendentals=0),
+        compiler_params=pltpu.CompilerParams(vmem_limit_bytes=8 << 20),
         grid_spec=pltpu.PrefetchScalarGridSpec(
             num_scalar_prefetch=1,
-            grid=(len(parts),),
+            grid=((stop - start) // bm,),
             in_specs=[
                 pl.BlockSpec((bm, rank), lambda i, half: (i + first, 0)),
                 pl.BlockSpec((rank, width), lambda i, half: (0, 0)),
-            ] + [RESIDENT] * len(parts) + [pl.BlockSpec(memory_space=pl.ANY)] * len(extra),
+                RESIDENT,
+                RESIDENT,
+            ] + [pl.BlockSpec(memory_space=pl.ANY)] * len(extra),
             out_specs=pl.BlockSpec((bm, width), lambda i, half: (i + first, half[0])),
             scratch_shapes=[pltpu.VMEM((2 * rank, width), BF16)],
         ),
-        out_shape=jax.ShapeDtypeStruct((rows, 2 * width), F32),
-        input_output_aliases={n_in - 1: 0} if extra else {},
-    )(half, left, right, *[near_core(part) for part in parts], *extra)
+        out_shape=jax.ShapeDtypeStruct((rows, n), F32),
+        input_output_aliases={5: 0} if extra else {},
+    )(half, left, right, near_core(momentum), near_core(gradient), *extra)
 
 
 def weight_kernel(count, half_ref, l_ref, a_ref, b_ref, s_ref, w_ref, o_ref, f_ref, split):
@@ -259,21 +261,26 @@
             split[:, pl.ds(start, width)] = along_swapped(factor, 0)
             f_ref[pl.ds(start, width), :] = factor.T
 
-    update = dot(along(l_ref[...], 1), split[...], NN)
-    o_ref[...] = w_ref[...] - 0.5 * update
+    left = along(l_ref[...], 1)
+    bm, n = o_ref.shape
+    here = pl.ds(pl.multiple_of(pl.program_id(0) * bm, bm), bm)
+    step = min(n, 512)
+    for c in range(0, n, step):
+        update = dot(left, split[:, c : c + step], NN)
+        o_ref[:, c : c + step] = w_ref[here, c : c + step] - 0.5 * update
 
 
 def weight_update(half, left, own, other, squares, weight, count):
     rows, n = weight.shape
     rank, width = own.shape
-    bm = tile(rows)
+    bm = tile(rows, 512)
     row = lambda i, half: (i, 0)
     still = lambda i, half: (0, 0)
     return pl.pallas_call(
         functools.partial(weight_kernel, float(count)),
         name="weight",
         cost_estimate=pl.CostEstimate(flops=6 * rows * n * rank, bytes_accessed=rows * n * 8, transcendentals=0),
-        compiler_params=pltpu.CompilerParams(vmem_limit_bytes=16 << 20),
+        compiler_params=pltpu.CompilerParams(vmem_limit_bytes=20 << 20),
         grid_spec=pltpu.PrefetchScalarGridSpec(
             num_scalar_prefetch=1,
             grid=(rows // bm,),
@@ -282,13 +289,16 @@
                 pl.BlockSpec((rank, width), still),
                 pl.BlockSpec((rank, width), still),
                 pl.BlockSpec(squares.shape, still),
-                pl.BlockSpec((bm, n), row),
+                RESIDENT,
             ],
             out_specs=(pl.BlockSpec((bm, n), row), pl.BlockSpec((n, rank), still)),
             scratch_shapes=[pltpu.VMEM((3 * rank, n), BF16)],
         ),
         out_shape=(jax.ShapeDtypeStruct((rows, n), F32), jax.ShapeDtypeStruct((n, rank), F32)),
     )(half, left, own, other, squares, near_core(weight))
+
+
+SHARES = (2, 2, 2, 2)
 
 
 class Axis:
@@ -331,11 +341,12 @@
     near = col.bits // 2
     order = tuple(range(col.bits))
     orders = (order, order[near:] + order[:near] if near == 0 else (near,) + tuple(b for b in order if b != near))
-    parts = 4
-    size = rows // parts
+    parts = len(SHARES)
+    sizes = [share * rows // sum(SHARES) for share in SHARES]
+    starts = [sum(sizes[:part]) for part in range(parts)]
     lefts, combined, cross, gram, right = [], [], None, None, right_factor
     for part in range(parts):
-        got = left_part(momentum, gradient, right, part == 0, part * size, size)
+        got = left_part(momentum, gradient, right, part == 0, starts[part], sizes[part])
         right = got[2] if part == 0 else right
         combined.append(got[1])
         lefts.append(col.total(got[0], orders[part % 2]))
@@ -360,13 +371,13 @@
     own, squares = right_side(inverse, cross + other)
     other = row.swap(own, 0)
     squares = row.exchange(squares, 0)
-    pieces = [(half, own, 0, parts), (1 - half, other, 0, parts // 2), (1 - half, other, parts // 2, parts)]
+    pieces = [(half, own, 0, rows), (1 - half, other, 0, rows // 2), (1 - half, other, rows // 2, rows)]
     new_momentum = None
     for bit in range(col.bits):
         squares = col.exchange(squares, bit)
         if bit < len(pieces):
             side, value, start, stop = pieces[bit]
-            new_momentum = momentum_half(side, left, value, combined[start:stop], start, new_momentum)
+            new_momentum = momentum_half(side, left, value, momentum, gradient, start, stop, new_momentum)
     new_weight, new_factor = weight_update(half, left, own, other, squares, weight, count)
     return new_weight, new_momentum, new_factor
 

time: 202 us -> 200 us (0.990)
  Pallas kernels: 85.6 us -> 80.3 us
  local copies, waits for them, and re-layouts: 8.39 us -> 12.3 us
    pallas_call x1, Pallas kernels: 27.5 us -> 22.8 us  [inverse_factor(): call(inverse_kernel, 12 * rank ** 3 * 20, rank * rank * 8, out_shape=jax....]
    unnamed x44 -> x46, local copies, waits for them, and re-layouts: 4.8 us -> 8.65 us
  transfers between devices with their start and end apart: 29 -> 29, of which waited for: 14 -> 14; matrix products, arithmetic and copies ran while one was open for 3% -> 3% of each run, Pallas kernels for 29% -> 27%
where the time goes in v2:
time: 200 us
  Pallas kernels  80.3 us (40%)
  waiting for transfers between devices  66.1 us (33%)
  starting transfers between devices  34.7 us (17%)
  local copies, waits for them, and re-layouts  12.3 us (6%)
  other arithmetic  5.38 us (3%)
    ppermute x29, waiting for transfers between devices, swap(): lax.ppermute(value, self.name, [(i, i ^ 1 << bit) for i in range(self.siz...  66.1 us
    ppermute x29, starting transfers between devices, swap(): lax.ppermute(value, self.name, [(i, i ^ 1 << bit) for i in range(self.siz...  34.7 us
    pallas_call x1, Pallas kernels, inverse_factor(): call(inverse_kernel, 12 * rank ** 3 * 20, rank * rank * 8, out_shape=jax....  22.8 us
    pallas_call x4, Pallas kernels, left_part(): call(functools.partial(left_kernel, opening), 6 * rows * n * rank, rows *...  19.9 us
    pallas_call x3, Pallas kernels, momentum_half(): pl.pallas_call(functools.partial(momentum_kernel, first), name='momentum'...  13.5 us
    pallas_call x1, Pallas kernels, weight_update(): pl.pallas_call(functools.partial(weight_kernel, float(count)), name='weig...  10.4 us
    unnamed x46, local copies, waits for them, and re-layouts  8.65 us
    pallas_call x4, Pallas kernels, cross_part(): call(cross_kernel, 6 * rows * n * rank, rank * n * 8, in_specs=[RESIDENT]...  7.97 us
  transfers between devices with their start and end apart: 29, of which 14 were waited for; matrix products, arithmetic and copies ran while one was open for 3% of the time, Pallas kernels for 27%

profile of v2, /device:TPU:0, one launch (start us, length us, event | category | flops | bytes accessed | tf_op | source)
XLA Modules:
  0.0 200.0 jit_solution(13766789598864158641)
XLA Ops:
  0.6 5.7 %shard_map.67 = (f32[512,256]{1,0:T(8,128)S(1)}, f32[512,2048]{1,0:T(8,128)}, bf16[6144,256]{1,0:T(8,128)(2,1)S(1)}) custom-call(f32[2048,2048]{1,0:T(8,128)} %m_ref.13, bf16[2048,2048]{1,0:T(8,128)(2,1)} %g_ref.13, f32[2048,256]{1,0:T(8,128)} %r_ref.1), custom_call_target="tpu_custom_call" | custom-call | flops 1610612736 | bytes 6291456 | tf_op jit(solution)/shard_map/pallas_call | solution.py:94
  7.2 3.0 %collective-permute-start = (f32[256,256]{1,0:T(8,128)S(1)}, f32[256,256]{1,0:T(8,128)}, u32[]{:S(2)}, u32[]{:S(2)}) collective-permute-start(f32[256,256]{1,0:T(8,128)S(1)} %constant_dynamic-slice_fusion.8), channel_id=1, source_target_pairs={{0,4},{4,0},{8,12},{12,8},{16,20},{20,16},{24,28},{28,24},{1,5},{5... | collective-permute-start | bytes 786440 | tf_op jit(solution)/shard_map/ppermute | solution.py:310
  10.2 4.7 %shard_map.70 = (f32[512,256]{1,0:T(8,128)S(1)}, f32[512,2048]{1,0:T(8,128)}) custom-call(f32[2048,2048]{1,0:T(8,128)} %m_ref.13, bf16[2048,2048]{1,0:T(8,128)(2,1)} %g_ref.13, bf16[6144,256]{1,0:T(8,128)(2,1)S(1)} %get-tuple-element.20.r_ref), custom_call_target="tpu_custom_call" | custom-call | flops 1610612736 | bytes 6291456 | tf_op jit(solution)/shard_map/pallas_call | solution.py:94
  15.7 1.7 constant_dynamic-slice_fusion.2
  18.9 4.7 %shard_map.69 = (f32[512,256]{1,0:T(8,128)S(1)}, f32[512,2048]{1,0:T(8,128)}) custom-call(f32[2048,2048]{1,0:T(8,128)} %m_ref.13, bf16[2048,2048]{1,0:T(8,128)(2,1)} %g_ref.13, bf16[6144,256]{1,0:T(8,128)(2,1)S(1)} %get-tuple-element.20.r_ref), custom_call_target="tpu_custom_call" | custom-call | flops 1610612736 | bytes 6291456 | tf_op jit(solution)/shard_map/pallas_call | solution.py:94
  25.1 4.7 %shard_map.68 = (f32[512,256]{1,0:T(8,128)S(1)}, f32[512,2048]{1,0:T(8,128)}) custom-call(f32[2048,2048]{1,0:T(8,128)} %m_ref.13, bf16[2048,2048]{1,0:T(8,128)(2,1)} %g_ref.13, bf16[6144,256]{1,0:T(8,128)(2,1)S(1)} %get-tuple-element.20.r_ref), custom_call_target="tpu_custom_call" | custom-call | flops 1610612736 | bytes 6291456 | tf_op jit(solution)/shard_map/pallas_call | solution.py:94
  31.9 2.0 %collective-permute-start.1 = (f32[128,256]{1,0:T(8,128)S(1)}, f32[128,256]{1,0:T(8,128)S(1)}, u32[]{:S(2)}, u32[]{:S(2)}) collective-permute-start(f32[128,256]{1,0:T(8,128)S(1)} %constant_dynamic-slice_fusion.7), channel_id=1, source_target_pairs={{0,8},{4,12},{8,0},{12,4},{16,24},{20,28},{24,16},{28,20},{1,9},{5... | collective-permute-start | bytes 393224 | tf_op jit(solution)/shard_map/ppermute | solution.py:310
  38.1 1.8 collective-permute-done.5
  42.2 3.2 %collective-permute-start.2 = (f32[128,256]{1,0:T(8,128)S(1)}, f32[128,256]{1,0:T(8,128)S(1)}, u32[]{:S(2)}, u32[]{:S(2)}) collective-permute-start(f32[128,256]{1,0:T(8,128)S(1)} %dynamic-slice_add_fusion.8), channel_id=1, source_target_pairs={{0,16},{4,20},{8,24},{12,28},{16,0},{20,4},{24,8},{28,12},{1,17},{... | collective-permute-start | bytes 393224 | tf_op jit(solution)/shard_map/ppermute | solution.py:310
  45.6 3.0 %collective-permute-start.12 = (f32[128,256]{1,0:T(8,128)S(1)}, f32[128,256]{1,0:T(8,128)S(1)}, u32[]{:S(2)}, u32[]{:S(2)}) collective-permute-start(f32[128,256]{1,0:T(8,128)S(1)} %dynamic-slice_add_fusion.6), channel_id=1, source_target_pairs={{0,16},{4,20},{8,24},{12,28},{16,0},{20,4},{24,8},{28,12},{1,17},{... | collective-permute-start | bytes 393224 | tf_op jit(solution)/shard_map/ppermute | solution.py:310
  48.7 10.8 %collective-permute-done.2 = f32[128,256]{1,0:T(8,128)S(1)} collective-permute-done((f32[128,256]{1,0:T(8,128)S(1)}, f32[128,256]{1,0:T(8,128)S(1)}, u32[]{:S(2)}, u32[]{:S(2)}) %collective-permute-start.2) | collective-permute-done | bytes 131104 | tf_op jit(solution)/shard_map/ppermute | solution.py:310
  59.6 4.5 %collective-permute-done.12 = f32[128,256]{1,0:T(8,128)S(1)} collective-permute-done((f32[128,256]{1,0:T(8,128)S(1)}, f32[128,256]{1,0:T(8,128)S(1)}, u32[]{:S(2)}, u32[]{:S(2)}) %collective-permute-start.12) | collective-permute-done | bytes 131104 | tf_op jit(solution)/shard_map/ppermute | solution.py:310
  72.2 3.3 %collective-permute-start.9 = (f32[256,256]{1,0:T(8,128)S(1)}, f32[256,256]{1,0:T(8,128)S(1)}, u32[]{:S(2)}, u32[]{:S(2)}) collective-permute-start(f32[256,256]{1,0:T(8,128)S(1)} %maximum_select_fusion.5), channel_id=1, source_target_pairs={{0,8},{4,12},{8,0},{12,4},{16,24},{20,28},{24,16},{28,20},{1,9},{5... | collective-permute-start | bytes 786440 | tf_op jit(solution)/shard_map/ppermute | solution.py:310
  75.6 2.2 %collective-permute-done.4 = f32[256,256]{1,0:T(8,128)S(1)} collective-permute-done((f32[256,256]{1,0:T(8,128)S(1)}, f32[256,256]{1,0:T(8,128)S(1)}, u32[]{:S(2)}, u32[]{:S(2)}) %collective-permute-start.4) | collective-permute-done | bytes 262176 | tf_op jit(solution)/shard_map/ppermute | solution.py:310
  77.9 4.0 %collective-permute-done.14 = f32[256,256]{1,0:T(8,128)S(1)} collective-permute-done((f32[256,256]{1,0:T(8,128)S(1)}, f32[256,256]{1,0:T(8,128)S(1)}, u32[]{:S(2)}, u32[]{:S(2)}) %collective-permute-start.14) | collective-permute-done | bytes 262176 | tf_op jit(solution)/shard_map/ppermute | solution.py:310
  84.2 1.9 shard_map.75.refs_0_
  86.9 2.0 %shard_map.76.refs_0_ = f32[256,2048]{1,0:T(8,128)S(1)} custom-call(f32[512,256]{1,0:T(8,128)S(1)} %maximum_select_fusion.1.refs_0_.l_ref, f32[512,2048]{1,0:T(8,128)S(1)} %copy-done.6, f32[256,2048]{1,0:T(8,128)S(1)} %shard_map.75.refs_0_), custom_call_target="tpu_custom_call", output_to_operand_aliasing={{}: (2, {})} | custom-call | flops 1610612736 | bytes 4194304 | tf_op jit(solution)/shard_map/pallas_call | solution.py:117
  89.1 2.0 %shard_map.77.refs_0_ = f32[256,2048]{1,0:T(8,128)S(1)} custom-call(f32[512,256]{1,0:T(8,128)S(1)} %maximum_select_fusion.2.refs_0_.l_ref, f32[512,2048]{1,0:T(8,128)S(1)} %copy-done.5, f32[256,2048]{1,0:T(8,128)S(1)} %shard_map.76.refs_0_), custom_call_target="tpu_custom_call", output_to_operand_aliasing={{}: (2, {})} | custom-call | flops 1610612736 | bytes 4194304 | tf_op jit(solution)/shard_map/pallas_call | solution.py:117
  91.3 2.0 %shard_map.78 = f32[256,2048]{1,0:T(8,128)S(1)} custom-call(f32[512,256]{1,0:T(8,128)S(1)} %maximum_select_fusion.3.refs_0_.l_ref, f32[512,2048]{1,0:T(8,128)S(1)} %copy-done.4, f32[256,2048]{1,0:T(8,128)S(1)} %shard_map.77.refs_0_), custom_call_target="tpu_custom_call", output_to_operand_aliasing={{}: (2, {})} | custom-call | flops 1610612736 | bytes 4194304 | tf_op jit(solution)/shard_map/pallas_call | solution.py:117
  94.8 2.6 %collective-permute-done.22 = f32[256,1024]{1,0:T(8,128)} collective-permute-done((f32[256,1024]{1,0:T(8,128)}, f32[256,1024]{1,0:T(8,128)}, u32[]{:S(2)}, u32[]{:S(2)}) %collective-permute-start.22) | collective-permute-done | bytes 1048608 | tf_op jit(solution)/shard_map/ppermute | solution.py:310
  100.9 29.0 %collective-permute-done.21 = f32[256,256]{1,0:T(8,128)S(1)} collective-permute-done((f32[256,256]{1,0:T(8,128)S(1)}, f32[256,256]{1,0:T(8,128)S(1)}, u32[]{:S(2)}, u32[]{:S(2)}) %collective-permute-start.21) | collective-permute-done | bytes 262176 | tf_op jit(solution)/shard_map/ppermute | solution.py:310
  130.1 22.8 %shard_map.79.x_ref = f32[256,256]{1,0:T(8,128)S(1)} custom-call(f32[256,256]{1,0:T(8,128)S(1)} %add.119.g_ref), custom_call_target="tpu_custom_call" | custom-call | flops 4026531840 | bytes 524288 | tf_op jit(solution)/shard_map/pallas_call | solution.py:173
  154.8 2.3 %collective-permute-done.25 = f32[256,128]{1,0:T(8,128)S(1)} collective-permute-done((f32[256,128]{1,0:T(8,128)S(1)}, f32[256,128]{1,0:T(8,128)S(1)}, u32[]{:S(2)}, u32[]{:S(2)}) %collective-permute-start.25) | collective-permute-done | bytes 131104 | tf_op jit(solution)/shard_map/ppermute | solution.py:310
  158.9 3.9 %collective-permute-done.26 = f32[256,128]{1,0:T(8,128)S(1)} collective-permute-done((f32[256,128]{1,0:T(8,128)S(1)}, f32[256,128]{1,0:T(8,128)S(1)}, u32[]{:S(2)}, u32[]{:S(2)}) %collective-permute-start.26) | collective-permute-done | bytes 131104 | tf_op jit(solution)/shard_map/ppermute | solution.py:310
  163.7 1.8 shard_map.80.l_ref
  165.5 2.3 %collective-permute-done.27 = f32[256,128]{1,0:T(8,128)S(1)} collective-permute-done((f32[256,128]{1,0:T(8,128)S(1)}, f32[256,128]{1,0:T(8,128)S(1)}, u32[]{:S(2)}, u32[]{:S(2)}) %collective-permute-start.27) | collective-permute-done | bytes 131104 | tf_op jit(solution)/shard_map/ppermute | solution.py:310
  167.8 2.4 %collective-permute-start.28 = (f32[256,128]{1,0:T(8,128)S(1)}, f32[256,128]{1,0:T(8,128)S(1)}, u32[]{:S(2)}, u32[]{:S(2)}) collective-permute-start(f32[256,128]{1,0:T(8,128)S(1)} %add.126), channel_id=1, source_target_pairs={{0,16},{4,20},{8,24},{12,28},{16,0},{20,4},{24,8},{28,12},{1,17},{... | collective-permute-start | bytes 393224 | tf_op jit(solution)/shard_map/ppermute | solution.py:310
  170.3 6.3 %momentum.3.refs_0_ = f32[2048,2048]{1,0:T(8,128)} custom-call(s32[1]{0:T(128)} %bitcast.half_ref, f32[2048,256]{1,0:T(8,128)S(1)} %shard_map.80.l_ref, f32[256,1024]{1,0:T(8,128)S(1)} %get-tuple-element.31.a_ref.r_ref, f32[2048,2048]{1,0:T(8,128)S(1)} %bitcast.2, bf16[2048,2048]{1,0:T(8,128)(2,1)S(1)} %bitcast.4), custom_call_target="tpu_custom_call" | custom-call | flops 2147483648 | bytes 8388608 | tf_op jit(solution)/shard_map/momentum/pallas_call | solution.py:231
  176.6 3.7 %momentum.4.refs_0_ = f32[2048,2048]{1,0:T(8,128)} custom-call(s32[1]{0:T(128)S(6)} %sub.22.half_ref, f32[2048,256]{1,0:T(8,128)S(1)} %shard_map.80.l_ref, f32[256,1024]{1,0:T(8,128)S(1)} %collective-permute-done.24.b_ref.r_ref, f32[2048,2048]{1,0:T(8,128)S(1)} %bitcast.2, bf16[2048,2048]{1,0:T(8,128)(2,1)S(1)} %bitcast.4, ...), custom_call_target="tpu_custom_call", output_to_operand_aliasing={{}: (5, {})} | custom-call | flops 1073741824 | bytes 4194304 | tf_op jit(solution)/shard_map/momentum/pallas_call | solution.py:231
  180.4 3.4 %momentum.5 = f32[2048,2048]{1,0:T(8,128)} custom-call(s32[1]{0:T(128)S(6)} %sub.22.half_ref, f32[2048,256]{1,0:T(8,128)S(1)} %shard_map.80.l_ref, f32[256,1024]{1,0:T(8,128)S(1)} %collective-permute-done.24.b_ref.r_ref, f32[2048,2048]{1,0:T(8,128)S(1)} %bitcast.2, bf16[2048,2048]{1,0:T(8,128)(2,1)S(1)} %bitcast.4, ...), custom_call_target="tpu_custom_call", output_to_operand_aliasing={{}: (5, {})} | custom-call | flops 1073741824 | bytes 4194304 | tf_op jit(solution)/shard_map/momentum/pallas_call | solution.py:231
  183.8 5.8 %copy-done.16 = f32[2048,2048]{1,0:T(8,128)S(1)} copy-done((f32[2048,2048]{1,0:T(8,128)S(1)}, f32[2048,2048]{1,0:T(8,128)}, u32[]{:S(2)}) %copy-start.16) | copy-done | bytes 16777240
  189.6 10.4 %weight.1 = (f32[2048,2048]{1,0:T(8,128)}, f32[2048,256]{1,0:T(8,128)}) custom-call(s32[1]{0:T(128)} %bitcast.half_ref, f32[2048,256]{1,0:T(8,128)S(1)} %shard_map.80.l_ref, f32[256,1024]{1,0:T(8,128)S(1)} %copy-done.9, f32[256,1024]{1,0:T(8,128)S(1)} %collective-permute-done.24.b_ref.r_ref, f32[256,128]{1,0:T(8,128)S(1)} %add.127.s_ref, ...), custom_call_target="tpu_custom_call" | custom-call | flops 6442450944 | bytes 33554432 | tf_op jit(solution)/shard_map/weight/pallas_call | solution.py:279
  (131 shorter events, 34.6 us)
Async XLA Ops:
  7.2 23.6 %collective-permute-start = (f32[256,256]{1,0:T(8,128)S(1)}, f32[256,256]{1,0:T(8,128)}, u32[]{:S(2)}, u32[]{:S(2)}) collective-permute-start(f32[256,256]{1,0:T(8,128)S(1)} %constant_dynamic-slice_fusion.8), channel_id=1, source_target_pairs={{0,4},{4,0},{8,12},{12,8},{16,20},{20,16},{24,28},{28,24},{1,5},{5... | collective-permute-start | bytes 786440 | tf_op jit(solution)/shard_map/ppermute | solution.py:310
  17.4 16.6 %collective-permute-start.15 = (f32[256,256]{1,0:T(8,128)}, f32[256,256]{1,0:T(8,128)}, u32[]{:S(2)}, u32[]{:S(2)}) collective-permute-start(f32[256,256]{1,0:T(8,128)} %constant_dynamic-slice_fusion.2), channel_id=1, source_target_pairs={{0,8},{4,12},{8,0},{12,4},{16,24},{20,28},{24,16},{28,20},{1,9},{5... | collective-permute-start | bytes 786440 | tf_op jit(solution)/shard_map/ppermute | solution.py:310
  24.6 12.1 %collective-permute-start.10 = (f32[256,256]{1,0:T(8,128)}, f32[256,256]{1,0:T(8,128)}, u32[]{:S(2)}, u32[]{:S(2)}) collective-permute-start(f32[256,256]{1,0:T(8,128)} %constant_dynamic-slice_fusion.4), channel_id=1, source_target_pairs={{0,4},{4,0},{8,12},{12,8},{16,20},{20,16},{24,28},{28,24},{1,5},{5... | collective-permute-start | bytes 786440 | tf_op jit(solution)/shard_map/ppermute | solution.py:310
  30.7 9.2 %collective-permute-start.5 = (f32[256,256]{1,0:T(8,128)S(1)}, f32[256,256]{1,0:T(8,128)S(1)}, u32[]{:S(2)}, u32[]{:S(2)}) collective-permute-start(f32[256,256]{1,0:T(8,128)S(1)} %constant_dynamic-slice_fusion.6), channel_id=1, source_target_pairs={{0,8},{4,12},{8,0},{12,4},{16,24},{20,28},{24,16},{28,20},{1,9},{5... | collective-permute-start | bytes 786440 | tf_op jit(solution)/shard_map/ppermute | solution.py:310
  31.9 10.2 %collective-permute-start.1 = (f32[128,256]{1,0:T(8,128)S(1)}, f32[128,256]{1,0:T(8,128)S(1)}, u32[]{:S(2)}, u32[]{:S(2)}) collective-permute-start(f32[128,256]{1,0:T(8,128)S(1)} %constant_dynamic-slice_fusion.7), channel_id=1, source_target_pairs={{0,8},{4,12},{8,0},{12,4},{16,24},{20,28},{24,16},{28,20},{1,9},{5... | collective-permute-start | bytes 393224 | tf_op jit(solution)/shard_map/ppermute | solution.py:310
  35.1 10.4 %collective-permute-start.16 = (f32[128,256]{1,0:T(8,128)S(1)}, f32[128,256]{1,0:T(8,128)S(1)}, u32[]{:S(2)}, u32[]{:S(2)}) collective-permute-start(f32[128,256]{1,0:T(8,128)S(1)} %constant_dynamic-slice_fusion.1), channel_id=1, source_target_pairs={{0,4},{4,0},{8,12},{12,8},{16,20},{20,16},{24,28},{28,24},{1,5},{5... | collective-permute-start | bytes 393224 | tf_op jit(solution)/shard_map/ppermute | solution.py:310
  37.6 7.9 %collective-permute-start.11 = (f32[128,256]{1,0:T(8,128)S(1)}, f32[128,256]{1,0:T(8,128)S(1)}, u32[]{:S(2)}, u32[]{:S(2)}) collective-permute-start(f32[128,256]{1,0:T(8,128)S(1)} %constant_dynamic-slice_fusion.3), channel_id=1, source_target_pairs={{0,8},{4,12},{8,0},{12,4},{16,24},{20,28},{24,16},{28,20},{1,9},{5... | collective-permute-start | bytes 393224 | tf_op jit(solution)/shard_map/ppermute | solution.py:310
  40.0 8.5 %collective-permute-start.6 = (f32[128,256]{1,0:T(8,128)S(1)}, f32[128,256]{1,0:T(8,128)S(1)}, u32[]{:S(2)}, u32[]{:S(2)}) collective-permute-start(f32[128,256]{1,0:T(8,128)S(1)} %constant_dynamic-slice_fusion.5), channel_id=1, source_target_pairs={{0,4},{4,0},{8,12},{12,8},{16,20},{20,16},{24,28},{28,24},{1,5},{5... | collective-permute-start | bytes 393224 | tf_op jit(solution)/shard_map/ppermute | solution.py:310
  42.2 17.2 %collective-permute-start.2 = (f32[128,256]{1,0:T(8,128)S(1)}, f32[128,256]{1,0:T(8,128)S(1)}, u32[]{:S(2)}, u32[]{:S(2)}) collective-permute-start(f32[128,256]{1,0:T(8,128)S(1)} %dynamic-slice_add_fusion.8), channel_id=1, source_target_pairs={{0,16},{4,20},{8,24},{12,28},{16,0},{20,4},{24,8},{28,12},{1,17},{... | collective-permute-start | bytes 393224 | tf_op jit(solution)/shard_map/ppermute | solution.py:310
  45.5 18.7 %collective-permute-start.17 = (f32[128,256]{1,0:T(8,128)S(1)}, f32[128,256]{1,0:T(8,128)S(1)}, u32[]{:S(2)}, u32[]{:S(2)}) collective-permute-start(f32[128,256]{1,0:T(8,128)S(1)} %dynamic-slice_add_fusion.5), channel_id=1, source_target_pairs={{0,16},{4,20},{8,24},{12,28},{16,0},{20,4},{24,8},{28,12},{1,17},{... | collective-permute-start | bytes 393224 | tf_op jit(solution)/shard_map/ppermute | solution.py:310
  45.6 18.5 %collective-permute-start.12 = (f32[128,256]{1,0:T(8,128)S(1)}, f32[128,256]{1,0:T(8,128)S(1)}, u32[]{:S(2)}, u32[]{:S(2)}) collective-permute-start(f32[128,256]{1,0:T(8,128)S(1)} %dynamic-slice_add_fusion.6), channel_id=1, source_target_pairs={{0,16},{4,20},{8,24},{12,28},{16,0},{20,4},{24,8},{28,12},{1,17},{... | collective-permute-start | bytes 393224 | tf_op jit(solution)/shard_map/ppermute | solution.py:310
  48.6 17.2 %collective-permute-start.7 = (f32[128,256]{1,0:T(8,128)S(1)}, f32[128,256]{1,0:T(8,128)S(1)}, u32[]{:S(2)}, u32[]{:S(2)}) collective-permute-start(f32[128,256]{1,0:T(8,128)S(1)} %dynamic-slice_add_fusion.7), channel_id=1, source_target_pairs={{0,16},{4,20},{8,24},{12,28},{16,0},{20,4},{24,8},{28,12},{1,17},{... | collective-permute-start | bytes 393224 | tf_op jit(solution)/shard_map/ppermute | solution.py:310
  59.5 8.8 %collective-permute-start.3 = (f32[128,256]{1,0:T(8,128)S(1)}, f32[128,256]{1,0:T(8,128)S(1)}, u32[]{:S(2)}, u32[]{:S(2)}) collective-permute-start(f32[128,256]{1,0:T(8,128)S(1)} %add.104), channel_id=1, source_target_pairs={{0,8},{4,12},{8,0},{12,4},{16,24},{20,28},{24,16},{28,20},{1,9},{5... | collective-permute-start | bytes 393224 | tf_op jit(solution)/shard_map/ppermute | solution.py:310
  64.1 6.0 %collective-permute-start.13 = (f32[128,256]{1,0:T(8,128)S(1)}, f32[128,256]{1,0:T(8,128)S(1)}, u32[]{:S(2)}, u32[]{:S(2)}) collective-permute-start(f32[128,256]{1,0:T(8,128)S(1)} %add.114), channel_id=1, source_target_pairs={{0,8},{4,12},{8,0},{12,4},{16,24},{20,28},{24,16},{28,20},{1,9},{5... | collective-permute-start | bytes 393224 | tf_op jit(solution)/shard_map/ppermute | solution.py:310
  64.2 11.3 %collective-permute-start.18 = (f32[128,256]{1,0:T(8,128)S(1)}, f32[128,256]{1,0:T(8,128)S(1)}, u32[]{:S(2)}, u32[]{:S(2)}) collective-permute-start(f32[128,256]{1,0:T(8,128)S(1)} %add.117), channel_id=1, source_target_pairs={{0,4},{4,0},{8,12},{12,8},{16,20},{20,16},{24,28},{28,24},{1,5},{5... | collective-permute-start | bytes 393224 | tf_op jit(solution)/shard_map/ppermute | solution.py:310
  65.8 6.4 %collective-permute-start.8 = (f32[128,256]{1,0:T(8,128)S(1)}, f32[128,256]{1,0:T(8,128)S(1)}, u32[]{:S(2)}, u32[]{:S(2)}) collective-permute-start(f32[128,256]{1,0:T(8,128)S(1)} %add.111), channel_id=1, source_target_pairs={{0,4},{4,0},{8,12},{12,8},{16,20},{20,16},{24,28},{28,24},{1,5},{5... | collective-permute-start | bytes 393224 | tf_op jit(solution)/shard_map/ppermute | solution.py:310
  68.3 9.6 %collective-permute-start.4 = (f32[256,256]{1,0:T(8,128)S(1)}, f32[256,256]{1,0:T(8,128)S(1)}, u32[]{:S(2)}, u32[]{:S(2)}) collective-permute-start(f32[256,256]{1,0:T(8,128)S(1)} %maximum_select_fusion.4), channel_id=1, source_target_pairs={{0,4},{4,0},{8,12},{12,8},{16,20},{20,16},{24,28},{28,24},{1,5},{5... | collective-permute-start | bytes 786440 | tf_op jit(solution)/shard_map/ppermute | solution.py:310
  70.1 11.7 %collective-permute-start.14 = (f32[256,256]{1,0:T(8,128)S(1)}, f32[256,256]{1,0:T(8,128)S(1)}, u32[]{:S(2)}, u32[]{:S(2)}) collective-permute-start(f32[256,256]{1,0:T(8,128)S(1)} %maximum_select_fusion.6), channel_id=1, source_target_pairs={{0,4},{4,0},{8,12},{12,8},{16,20},{20,16},{24,28},{28,24},{1,5},{5... | collective-permute-start | bytes 786440 | tf_op jit(solution)/shard_map/ppermute | solution.py:310
  72.2 9.7 %collective-permute-start.9 = (f32[256,256]{1,0:T(8,128)S(1)}, f32[256,256]{1,0:T(8,128)S(1)}, u32[]{:S(2)}, u32[]{:S(2)}) collective-permute-start(f32[256,256]{1,0:T(8,128)S(1)} %maximum_select_fusion.5), channel_id=1, source_target_pairs={{0,8},{4,12},{8,0},{12,4},{16,24},{20,28},{24,16},{28,20},{1,9},{5... | collective-permute-start | bytes 786440 | tf_op jit(solution)/shard_map/ppermute | solution.py:310
  75.5 10.5 %collective-permute-start.19 = (f32[256,256]{1,0:T(8,128)S(1)}, f32[256,256]{1,0:T(8,128)S(1)}, u32[]{:S(2)}, u32[]{:S(2)}) collective-permute-start(f32[256,256]{1,0:T(8,128)S(1)} %maximum_select_fusion.7), channel_id=1, source_target_pairs={{0,8},{4,12},{8,0},{12,4},{16,24},{20,28},{24,16},{28,20},{1,9},{5... | collective-permute-start | bytes 786440 | tf_op jit(solution)/shard_map/ppermute | solution.py:310
  86.8 4.3 %collective-permute-start.20 = (f32[256,256]{1,0:T(8,128)S(1)}, f32[256,256]{1,0:T(8,128)S(1)}, u32[]{:S(2)}, u32[]{:S(2)}) collective-permute-start(f32[256,256]{1,0:T(8,128)S(1)} %shard_map.74), channel_id=1, source_target_pairs={{0,1},{1,0},{2,3},{3,2},{4,5},{5,4},{6,7},{7,6},{8,9},{9,8},{10,11... | collective-permute-start | bytes 786440 | tf_op jit(solution)/shard_map/ppermute | solution.py:310
  94.4 3.1 %collective-permute-start.22 = (f32[256,1024]{1,0:T(8,128)}, f32[256,1024]{1,0:T(8,128)}, u32[]{:S(2)}, u32[]{:S(2)}) collective-permute-start(f32[256,1024]{1,0:T(8,128)} %constant_dynamic-slice_fusion), channel_id=1, source_target_pairs={{0,1},{1,0},{2,3},{3,2},{4,5},{5,4},{6,7},{7,6},{8,9},{9,8},{10,11... | collective-permute-start | bytes 3145736 | tf_op jit(solution)/shard_map/ppermute | solution.py:310
  98.8 54.1 %collective-permute-start.23 = (f32[256,1024]{1,0:T(8,128)S(1)}, f32[256,1024]{1,0:T(8,128)S(1)}, u32[]{:S(2)}, u32[]{:S(2)}) collective-permute-start(f32[256,1024]{1,0:T(8,128)S(1)} %dynamic-slice_add_fusion), channel_id=1, source_target_pairs={{0,2},{1,3},{2,0},{3,1},{4,6},{5,7},{6,4},{7,5},{8,10},{9,11},{10,... | collective-permute-start | bytes 3145736 | tf_op jit(solution)/shard_map/ppermute | solution.py:310
  100.4 29.5 %collective-permute-start.21 = (f32[256,256]{1,0:T(8,128)S(1)}, f32[256,256]{1,0:T(8,128)S(1)}, u32[]{:S(2)}, u32[]{:S(2)}) collective-permute-start(f32[256,256]{1,0:T(8,128)S(1)} %add.118), channel_id=1, source_target_pairs={{0,2},{1,3},{2,0},{3,1},{4,6},{5,7},{6,4},{7,5},{8,10},{9,11},{10,... | collective-permute-start | bytes 786440 | tf_op jit(solution)/shard_map/ppermute | solution.py:310
  130.0 40.2 %slice-start = ((s8[16777216]{0:T(1024)(128)(4,1)}), s8[4194304]{0:T(1024)(128)(4,1)S(1)}, s32[]{:S(2)}) async-start(s8[16777216]{0:T(1024)(128)(4,1)} %bitcast.1), calls=%async_computation | async-start | bytes 8388608
  130.0 40.2 %slice-start.1 = ((s8[16777216]{0:T(1024)(128)(4,1)}), s8[4194304]{0:T(1024)(128)(4,1)S(1)}, s32[]{:S(2)}) async-start(s8[16777216]{0:T(1024)(128)(4,1)} %bitcast.1), calls=%async_computation.1 | async-start | bytes 8388608
  130.0 40.2 %slice-start.4 = ((s8[8388608]{0:T(1024)(128)(4,1)}), s8[4194304]{0:T(1024)(128)(4,1)S(1)}, s32[]{:S(2)}) async-start(s8[8388608]{0:T(1024)(128)(4,1)} %bitcast.3), calls=%async_computation.4 | async-start | bytes 8388608
  154.2 22.4 %collective-permute-start.24 = (f32[256,1024]{1,0:T(8,128)S(1)}, f32[256,1024]{1,0:T(8,128)S(1)}, u32[]{:S(2)}, u32[]{:S(2)}) collective-permute-start(f32[256,1024]{1,0:T(8,128)S(1)} %get-tuple-element.31.a_ref.r_ref), channel_id=1, source_target_pairs={{0,1},{1,0},{2,3},{3,2},{4,5},{5,4},{6,7},{7,6},{8,9},{9,8},{10,11... | collective-permute-start | bytes 3145736 | tf_op jit(solution)/shard_map/ppermute | solution.py:310
  154.3 2.8 %collective-permute-start.25 = (f32[256,128]{1,0:T(8,128)S(1)}, f32[256,128]{1,0:T(8,128)S(1)}, u32[]{:S(2)}, u32[]{:S(2)}) collective-permute-start(f32[256,128]{1,0:T(8,128)S(1)} %get-tuple-element.32), channel_id=1, source_target_pairs={{0,1},{1,0},{2,3},{3,2},{4,5},{5,4},{6,7},{7,6},{8,9},{9,8},{10,11... | collective-permute-start | bytes 393224 | tf_op jit(solution)/shard_map/ppermute | solution.py:310
  157.2 5.6 %collective-permute-start.26 = (f32[256,128]{1,0:T(8,128)S(1)}, f32[256,128]{1,0:T(8,128)S(1)}, u32[]{:S(2)}, u32[]{:S(2)}) collective-permute-start(f32[256,128]{1,0:T(8,128)S(1)} %add.124), channel_id=1, source_target_pairs={{0,4},{4,0},{8,12},{12,8},{16,20},{20,16},{24,28},{28,24},{1,5},{5... | collective-permute-start | bytes 393224 | tf_op jit(solution)/shard_map/ppermute | solution.py:310
  162.8 5.0 %collective-permute-start.27 = (f32[256,128]{1,0:T(8,128)S(1)}, f32[256,128]{1,0:T(8,128)S(1)}, u32[]{:S(2)}, u32[]{:S(2)}) collective-permute-start(f32[256,128]{1,0:T(8,128)S(1)} %add.125), channel_id=1, source_target_pairs={{0,8},{4,12},{8,0},{12,4},{16,24},{20,28},{24,16},{28,20},{1,9},{5... | collective-permute-start | bytes 393224 | tf_op jit(solution)/shard_map/ppermute | solution.py:310
  167.8 8.8 %collective-permute-start.28 = (f32[256,128]{1,0:T(8,128)S(1)}, f32[256,128]{1,0:T(8,128)S(1)}, u32[]{:S(2)}, u32[]{:S(2)}) collective-permute-start(f32[256,128]{1,0:T(8,128)S(1)} %add.126), channel_id=1, source_target_pairs={{0,16},{4,20},{8,24},{12,28},{16,0},{20,4},{24,8},{28,12},{1,17},{... | collective-permute-start | bytes 393224 | tf_op jit(solution)/shard_map/ppermute | solution.py:310
  (20 other events, 170.5 us)
